TPU v7x, 768 devices: a whole 4x8x12 slice. The times are simulated.
768 devices in a mesh: sec: 12 (over x, z_hi), lat: 64 (over z_lo, y, core).
Axes of the slice: x: 4, y: 8, z: 12 (z_hi: 3, z_lo: 4; z = z_hi * 4 + z_lo), core: 2. Of those that a mesh axis runs over, the one named last changes fastest.
Arguments:
- spectra: float32 [256, 288, 768], P('lat', 'sec'), may hold values from 0.2 to 2
- turning: float32 [256, 288], P('lat', 'sec'), may hold values from -0.45 to 0.45
- currents: float32 [256, 288, 64], P('lat', 'sec'), may hold values from -3 to 3
- drag_rates: float32 [32], replicated, may hold values from 0.02 to 0.3
- land_mask: int32 [256, 288], P('lat', 'sec'), may hold values 0 or 1
- ocean_target: int32 [256, 288], P('lat', 'sec'), may hold values from 0 to 11, as said below
Outputs:
- spectra_out: float32 [256, 288, 768], P('lat', 'sec')
- currents_out: float32 [256, 288, 64], P('lat', 'sec')
Inputs may be any that keep to these rules, and one draw needn't show every extreme that they name: `ocean_target`: in each device's block of 4 x 24 columns every target value appears on exactly 8 columns.
All inputs are finite; a program needn't handle non-finite values. No bound on the sum of `land_mask` on one device may be relied on, other than what follows from the above.
Results may differ from a plain program's by a relative error of at most 0.0003.
Values sent between devices are 32-bit elements; how exact they have to be, the bound alone decides.
A program may use at most 32 MiB of HBM per device.

v0:
```python
import math

import jax
import jax.numpy as jnp
from jax import lax
from jax.sharding import PartitionSpec as P

NFREQ = 24
NDIR = 32
STEPS = 3


stokes_scale = 0.1
ocean_dt = 0.3
current_gain = 0.2


def with_halo(cells, sides, width):
    for axis, dim in sides:
        count = lax.axis_size(axis)
        ends = count - 1
        head = lax.slice_in_dim(cells, 0, width, axis=dim)
        tail = lax.slice_in_dim(cells, cells.shape[dim] - width, cells.shape[dim], axis=dim)
        cells = jnp.concatenate(
            [
                lax.ppermute(tail, axis, [(i, (i + 1) % count) for i in range(ends)]),
                cells,
                lax.ppermute(head, axis, [((i + 1) % count, i) for i in range(ends)]),
            ],
            axis=dim,
        )
    return cells


def build_tables(nfreq, ndir, ndepth):
    fraction = jnp.arange(nfreq, dtype=jnp.float32) / (nfreq - 1)
    angles = (jnp.arange(ndir, dtype=jnp.float32) + 0.5) * (2.0 * math.pi / ndir)
    east_part = jnp.cos(angles)
    north_part = jnp.sin(angles)
    courant = 0.1 + 0.3 * fraction
    levels = jnp.arange(ndepth, dtype=jnp.float32)
    depth_level = 0.5 + (ndepth - 2) * (1.0 - fraction)
    weights = jnp.maximum(1.0 - jnp.abs(levels[None, :] - depth_level[:, None]), 0.0)
    mean_weights = weights / jnp.sum(weights, axis=1, keepdims=True)
    x_rate = (courant[:, None] * east_part[None, :]).reshape(-1)
    y_rate = (courant[:, None] * north_part[None, :]).reshape(-1)
    compass = jnp.stack([east_part, north_part])
    eye_freq = jnp.eye(nfreq, dtype=jnp.float32)
    eye_two = jnp.eye(2, dtype=jnp.float32)
    stokes_matrix = (
        stokes_scale * weights[:, None, None, :] * compass.T[None, :, :, None]
    ).reshape(nfreq * ndir, 2 * ndepth)
    moment_matrix = (eye_freq[:, None, None, :] * compass.T[None, :, :, None]).reshape(
        nfreq * ndir, 2 * nfreq
    )
    profile_matrix = (stokes_scale * eye_two[:, None, :, None] * weights[None, :, None, :]).reshape(
        2 * nfreq, 2 * ndepth
    )
    average_matrix = (eye_two[:, None, :, None] * mean_weights.T[None, :, None, :]).reshape(
        2 * ndepth, 2 * nfreq
    )
    turn_gain = 1.0 - 0.5 * fraction
    growth = current_gain * (1.0 + fraction)
    return (
        east_part,
        north_part,
        x_rate,
        y_rate,
        stokes_matrix,
        moment_matrix,
        profile_matrix,
        average_matrix,
        turn_gain,
        growth,
    )


def upwind(center, west, east, south, north, x_rate, y_rate):
    along_x = jnp.maximum(x_rate, 0.0) * (center - west) + jnp.minimum(x_rate, 0.0) * (
        east - center
    )
    along_y = jnp.maximum(y_rate, 0.0) * (center - south) + jnp.minimum(y_rate, 0.0) * (
        north - center
    )
    return center - along_x - along_y


def turn_grow(
    advected, turning, current_eff, east_part, north_part, turn_gain, growth, nfreq, ndir
):
    layout = advected.shape
    spread = advected.reshape(layout[:-1] + (nfreq, ndir))
    turn_rate = turning[..., None, None] * turn_gain[:, None]
    behind = jnp.roll(spread, 1, axis=-1)
    forward = jnp.roll(spread, -1, axis=-1)
    turned = (
        spread
        - jnp.maximum(turn_rate, 0.0) * (spread - behind)
        - jnp.minimum(turn_rate, 0.0) * (forward - spread)
    )
    zonal = current_eff[..., :nfreq]
    meridional = current_eff[..., nfreq:]
    aligned = zonal[..., None] * east_part + meridional[..., None] * north_part
    grown = turned * (1.0 + growth[:, None] * aligned)
    return grown.reshape(layout)


def ocean_step(currents, padded, stokes, coriolis, keep, ndepth):
    zonal = currents[..., :ndepth]
    meridional = currents[..., ndepth:]
    shear = 0.5 * (padded[1:-1, 2:, ndepth:] - padded[1:-1, :-2, ndepth:]) - 0.5 * (
        padded[2:, 1:-1, :ndepth] - padded[:-2, 1:-1, :ndepth]
    )
    spin = coriolis[:, None, None] + shear
    new_zonal = keep * (zonal + ocean_dt * spin * (meridional + stokes[..., ndepth:]))
    new_merid = keep * (meridional - ocean_dt * spin * (zonal + stokes[..., :ndepth]))
    return jnp.concatenate([new_zonal, new_merid], axis=-1)


def couple(outgoing, homeward):
    return (
        lax.all_to_all(outgoing, "sec", split_axis=0, concat_axis=0, tiled=True),
        lax.all_to_all(homeward, "sec", split_axis=0, concat_axis=0, tiled=True),
    )


def neighbours(spectra):
    padded = with_halo(spectra, (("lat", 0), ("sec", 1)), 1)
    return (padded[1:-1, :-2], padded[1:-1, 2:], padded[:-2, 1:-1], padded[2:, 1:-1])


def per_device(spectra, turning, currents, drag_rates, land_mask, ocean_target):
    lat_rows, lon_cols, spectral = spectra.shape
    depth_count = drag_rates.shape[0]
    sections = lax.axis_size("sec")
    column_count = lat_rows * lon_cols
    (
        east_part,
        north_part,
        x_rate,
        y_rate,
        stokes_matrix,
        moment_matrix,
        profile_matrix,
        average_matrix,
        turn_gain,
        growth,
    ) = build_tables(NFREQ, NDIR, depth_count)
    order = jnp.argsort(ocean_target.reshape(-1), stable=True)
    inverse = jnp.argsort(order, stable=True)
    sea = land_mask.astype(jnp.float32)[..., None]
    keep = 1.0 - drag_rates
    global_rows = (lax.axis_index("lat") * lat_rows + jnp.arange(lat_rows, dtype=jnp.int32)).astype(
        jnp.float32
    )
    coriolis = 0.2 + 0.6 * global_rows / (lat_rows * lax.axis_size("lat"))
    highest = lax.Precision.HIGHEST
    for iteration in range(STEPS):
        flat_waves = spectra.reshape(column_count, spectral)
        flat_ocean = currents.reshape(column_count, 2 * depth_count)
        outgoing = jnp.dot(flat_waves, stokes_matrix, precision=highest)[order]
        arrived, returned = couple(outgoing.reshape(sections, -1), flat_ocean.reshape(sections, -1))
        arrived = arrived.reshape(column_count, -1)
        returned = returned.reshape(column_count, -1)[inverse]
        current_eff = jnp.dot(returned, average_matrix, precision=highest)
        west, east, south, north = neighbours(spectra)
        ocean_padded = with_halo(currents, (("lat", 0), ("sec", 1)), 1)
        advected = upwind(spectra, west, east, south, north, x_rate, y_rate)
        new_spectra = (
            turn_grow(
                advected,
                turning,
                current_eff.reshape(lat_rows, lon_cols, -1),
                east_part,
                north_part,
                turn_gain,
                growth,
                NFREQ,
                NDIR,
            )
            * sea
        )
        currents = (
            ocean_step(
                currents,
                ocean_padded,
                arrived.reshape(lat_rows, lon_cols, -1),
                coriolis,
                keep,
                depth_count,
            )
            * sea
        )
        spectra = new_spectra
    return (spectra, currents)


def solution(mesh):
    return jax.shard_map(
        per_device,
        mesh=mesh,
        in_specs=(
            P("lat", "sec", None),
            P("lat", "sec"),
            P("lat", "sec", None),
            P(),
            P("lat", "sec"),
            P("lat", "sec"),
        ),
        out_specs=(P("lat", "sec", None), P("lat", "sec", None)),
        check_vma=False,
    )
```

profile of v0, /device:TPU:64, one launch (start us, length us, event | category | flops | bytes accessed | tf_op | source)
XLA Modules:
  0.0 248.1 jit_solution(14728315200761423336)
XLA Ops:
  3.7 5.8 %collective-permute-start.1 = (f32[1,24,768]{2,1,0:T(8,128)S(1)}, f32[1,24,768]{2,1,0:T(8,128)S(1)}, u32[]{:S(2)}, u32[]{:S(2)}) collective-permute-start(f32[1,24,768]{2,1,0:T(8,128)S(1)} %get-tuple-element.31), channel_id=1, source_target_pairs={{1,0},{2,1},{3,2},{4,3},{5,4},{6,5},{7,6},{8,7},{9,8},{10,9},{11,1... | collective-permute-start | bytes 221192 | tf_op jit(solution)/shard_map/ppermute | solution.py:28
  10.9 15.5 %all-to-all-start = ((f32[12,1,512]{2,1,0:T(1,128)}), f32[12,1,512]{2,1,0:T(1,128)S(1)}, u32[]{:S(2)}, u32[]{:S(2)}) async-start(f32[12,1,512]{2,1,0:T(1,128)} %all_to_all.42), calls=%async_computation | async-start | bytes 49152 | tf_op jit(solution)/shard_map/all_to_all | solution.py:123
  29.1 5.8 %collective-permute-start.9 = (f32[1,24,64]{2,1,0:T(8,128)S(1)}, f32[1,24,64]{2,1,0:T(8,128)S(1)}, u32[]{:S(2)}, u32[]{:S(2)}) collective-permute-start(f32[1,24,64]{2,1,0:T(8,128)S(1)} %get-tuple-element.46), channel_id=1, source_target_pairs={{1,0},{2,1},{3,2},{4,3},{5,4},{6,5},{7,6},{8,7},{9,8},{10,9},{11,1... | collective-permute-start | bytes 18440 | tf_op jit(solution)/shard_map/ppermute | solution.py:28
  36.3 2.5 %sort.31 = (s32[96]{0:T(128)}, s32[96]{0:T(128)S(1)}) sort(s32[96]{0:T(128)S(1)} %reshape.366, s32[96]{0:T(128)S(1)} %iota.138), dimensions={0}, to_apply=%region_0.0 | sort | flops 672 | bytes 1536 | tf_op jit(solution)/shard_map/jit(argsort)/sort | solution.py:149
  38.8 2.5 %sort.32 = (s32[96]{0:T(128)}, s32[96]{0:T(128)S(1)}) sort(s32[96]{0:T(128)S(1)} %get-tuple-element.4, s32[96]{0:T(128)S(1)} %iota.139), dimensions={0}, to_apply=%region_1.0 | sort | flops 672 | bytes 1536 | tf_op jit(solution)/shard_map/jit(argsort)/sort | solution.py:150
  47.6 8.5 %collective-permute-start.11 = (f32[6,1,64]{2,1,0:T(1,128)S(1)}, f32[6,1,64]{2,1,0:T(1,128)S(1)}, u32[]{:S(2)}, u32[]{:S(2)}) collective-permute-start(f32[6,1,64]{2,1,0:T(1,128)S(1)} %get-tuple-element.37), channel_id=1, source_target_pairs={{0,64},{64,128},{128,192},{192,256},{256,320},{320,384},{384,448},... | collective-permute-start | bytes 4616 | tf_op jit(solution)/shard_map/ppermute | solution.py:26
  56.1 10.5 %all-to-all-start.1 = ((f32[12,1,512]{2,1,0:T(1,128)}), f32[12,1,512]{2,1,0:T(1,128)S(1)}, u32[]{:S(2)}, u32[]{:S(2)}) async-start(f32[12,1,512]{2,1,0:T(1,128)} %all_to_all.43), calls=%async_computation.1 | async-start | bytes 49152 | tf_op jit(solution)/shard_map/all_to_all | solution.py:122
  67.6 9.1 %all-to-all-done.1 = f32[12,1,512]{2,1,0:T(1,128)S(1)} async-done(((f32[12,1,512]{2,1,0:T(1,128)}), f32[12,1,512]{2,1,0:T(1,128)S(1)}, u32[]{:S(2)}, u32[]{:S(2)}) %all-to-all-start.1) | async-done | bytes 24608 | tf_op jit(solution)/shard_map/all_to_all | solution.py:122
  82.7 5.8 %collective-permute-start.17 = (f32[1,24,64]{2,1,0:T(8,128)S(1)}, f32[1,24,64]{2,1,0:T(8,128)S(1)}, u32[]{:S(2)}, u32[]{:S(2)}) collective-permute-start(f32[1,24,64]{2,1,0:T(8,128)S(1)} %get-tuple-element.44), channel_id=1, source_target_pairs={{1,0},{2,1},{3,2},{4,3},{5,4},{6,5},{7,6},{8,7},{9,8},{10,9},{11,1... | collective-permute-start | bytes 18440 | tf_op jit(solution)/shard_map/ppermute | solution.py:28
  88.5 4.9 %all-to-all-start.2 = ((f32[12,1,512]{2,1,0:T(1,128)}), f32[12,1,512]{2,1,0:T(1,128)}, u32[]{:S(2)}, u32[]{:S(2)}) async-start(f32[12,1,512]{2,1,0:T(1,128)} %mul.975), calls=%async_computation.2 | async-start | bytes 49152 | tf_op jit(solution)/shard_map/all_to_all | solution.py:123
  93.4 7.8 %collective-permute-start.2 = (f32[6,1,768]{2,1,0:T(1,128)S(1)}, f32[6,1,768]{2,1,0:T(1,128)S(1)}, u32[]{:S(2)}, u32[]{:S(2)}) collective-permute-start(f32[6,1,768]{2,1,0:T(1,128)S(1)} %get-tuple-element.24), channel_id=1, source_target_pairs={{0,64},{64,128},{128,192},{192,256},{256,320},{320,384},{384,448},... | collective-permute-start | bytes 55304 | tf_op jit(solution)/shard_map/ppermute | solution.py:26
  104.4 9.7 %collective-permute-start.19 = (f32[6,1,64]{2,1,0:T(1,128)}, f32[6,1,64]{2,1,0:T(1,128)}, u32[]{:S(2)}, u32[]{:S(2)}) collective-permute-start(f32[6,1,64]{2,1,0:T(1,128)} %get-tuple-element.35), channel_id=1, source_target_pairs={{0,64},{64,128},{128,192},{192,256},{256,320},{320,384},{384,448},... | collective-permute-start | bytes 4616 | tf_op jit(solution)/shard_map/ppermute | solution.py:26
  122.9 5.8 %collective-permute-start.5 = (f32[1,24,768]{2,1,0:T(8,128)S(1)}, f32[1,24,768]{2,1,0:T(8,128)S(1)}, u32[]{:S(2)}, u32[]{:S(2)}) collective-permute-start(f32[1,24,768]{2,1,0:T(8,128)S(1)} %get-tuple-element.29), channel_id=1, source_target_pairs={{1,0},{2,1},{3,2},{4,3},{5,4},{6,5},{7,6},{8,7},{9,8},{10,9},{11,1... | collective-permute-start | bytes 221192 | tf_op jit(solution)/shard_map/ppermute | solution.py:28
  128.7 10.0 %all-to-all-start.3 = ((f32[12,1,512]{2,1,0:T(1,128)}), f32[12,1,512]{2,1,0:T(1,128)S(1)}, u32[]{:S(2)}, u32[]{:S(2)}) async-start(f32[12,1,512]{2,1,0:T(1,128)} %all_to_all.44), calls=%async_computation.3 | async-start | bytes 49152 | tf_op jit(solution)/shard_map/all_to_all | solution.py:122
  143.4 5.5 %all-to-all-done.3 = f32[12,1,512]{2,1,0:T(1,128)S(1)} async-done(((f32[12,1,512]{2,1,0:T(1,128)}), f32[12,1,512]{2,1,0:T(1,128)S(1)}, u32[]{:S(2)}, u32[]{:S(2)}) %all-to-all-start.3) | async-done | bytes 24608 | tf_op jit(solution)/shard_map/all_to_all | solution.py:122
  153.4 5.8 %collective-permute-start.21 = (f32[1,24,64]{2,1,0:T(8,128)S(1)}, f32[1,24,64]{2,1,0:T(8,128)S(1)}, u32[]{:S(2)}, u32[]{:S(2)}) collective-permute-start(f32[1,24,64]{2,1,0:T(8,128)S(1)} %get-tuple-element.38), channel_id=1, source_target_pairs={{1,0},{2,1},{3,2},{4,3},{5,4},{6,5},{7,6},{8,7},{9,8},{10,9},{11,1... | collective-permute-start | bytes 18440 | tf_op jit(solution)/shard_map/ppermute | solution.py:28
  159.2 4.9 %all-to-all-start.4 = ((f32[12,1,512]{2,1,0:T(1,128)}), f32[12,1,512]{2,1,0:T(1,128)}, u32[]{:S(2)}, u32[]{:S(2)}) async-start(f32[12,1,512]{2,1,0:T(1,128)} %mul.976), calls=%async_computation.4 | async-start | bytes 49152 | tf_op jit(solution)/shard_map/all_to_all | solution.py:123
  164.2 7.8 %collective-permute-start.6 = (f32[6,1,768]{2,1,0:T(1,128)S(1)}, f32[6,1,768]{2,1,0:T(1,128)S(1)}, u32[]{:S(2)}, u32[]{:S(2)}) collective-permute-start(f32[6,1,768]{2,1,0:T(1,128)S(1)} %get-tuple-element.22), channel_id=1, source_target_pairs={{0,64},{64,128},{128,192},{192,256},{256,320},{320,384},{384,448},... | collective-permute-start | bytes 55304 | tf_op jit(solution)/shard_map/ppermute | solution.py:26
  175.1 9.7 %collective-permute-start.23 = (f32[6,1,64]{2,1,0:T(1,128)}, f32[6,1,64]{2,1,0:T(1,128)}, u32[]{:S(2)}, u32[]{:S(2)}) collective-permute-start(f32[6,1,64]{2,1,0:T(1,128)} %get-tuple-element.33), channel_id=1, source_target_pairs={{0,64},{64,128},{128,192},{192,256},{256,320},{320,384},{384,448},... | collective-permute-start | bytes 4616 | tf_op jit(solution)/shard_map/ppermute | solution.py:26
  197.7 5.8 %collective-permute-start.13 = (f32[1,24,768]{2,1,0:T(8,128)S(1)}, f32[1,24,768]{2,1,0:T(8,128)S(1)}, u32[]{:S(2)}, u32[]{:S(2)}) collective-permute-start(f32[1,24,768]{2,1,0:T(8,128)S(1)} %get-tuple-element.27), channel_id=1, source_target_pairs={{1,0},{2,1},{3,2},{4,3},{5,4},{6,5},{7,6},{8,7},{9,8},{10,9},{11,1... | collective-permute-start | bytes 221192 | tf_op jit(solution)/shard_map/ppermute | solution.py:28
  203.5 10.0 %all-to-all-start.5 = ((f32[12,1,512]{2,1,0:T(1,128)}), f32[12,1,512]{2,1,0:T(1,128)S(1)}, u32[]{:S(2)}, u32[]{:S(2)}) async-start(f32[12,1,512]{2,1,0:T(1,128)} %all_to_all.45), calls=%async_computation.5 | async-start | bytes 49152 | tf_op jit(solution)/shard_map/all_to_all | solution.py:122
  217.5 6.2 %all-to-all-done.5 = f32[12,1,512]{2,1,0:T(1,128)S(1)} async-done(((f32[12,1,512]{2,1,0:T(1,128)}), f32[12,1,512]{2,1,0:T(1,128)S(1)}, u32[]{:S(2)}, u32[]{:S(2)}) %all-to-all-start.5) | async-done | bytes 24608 | tf_op jit(solution)/shard_map/all_to_all | solution.py:122
  225.5 4.8 %collective-permute-start.14 = (f32[6,1,768]{2,1,0:T(1,128)S(1)}, f32[6,1,768]{2,1,0:T(1,128)S(1)}, u32[]{:S(2)}, u32[]{:S(2)}) collective-permute-start(f32[6,1,768]{2,1,0:T(1,128)S(1)} %get-tuple-element.20), channel_id=1, source_target_pairs={{0,64},{64,128},{128,192},{192,256},{256,320},{320,384},{384,448},... | collective-permute-start | bytes 55304 | tf_op jit(solution)/shard_map/ppermute | solution.py:26
  232.4 7.5 %collective-permute-done.15 = f32[6,1,768]{2,1,0:T(1,128)S(1)} collective-permute-done((f32[6,1,768]{2,1,0:T(1,128)S(1)}, f32[6,1,768]{2,1,0:T(1,128)S(1)}, u32[]{:S(2)}, u32[]{:S(2)}) %collective-permute-start.15) | collective-permute-done | bytes 18464 | tf_op jit(solution)/shard_map/ppermute | solution.py:28
  (260 shorter events, 74.4 us)
Async XLA Ops:
  1.6 91.7 %collective-permute-start = (f32[1,24,768]{2,1,0:T(8,128)S(1)}, f32[1,24,768]{2,1,0:T(8,128)S(1)}, u32[]{:S(2)}, u32[]{:S(2)}) collective-permute-start(f32[1,24,768]{2,1,0:T(8,128)S(1)} %get-tuple-element.30), channel_id=1, source_target_pairs={{0,1},{1,2},{2,3},{3,4},{4,5},{5,6},{6,7},{7,8},{8,9},{9,10},{10,1... | collective-permute-start | bytes 221192 | tf_op jit(solution)/shard_map/ppermute | solution.py:26
  3.7 89.7 %collective-permute-start.1 = (f32[1,24,768]{2,1,0:T(8,128)S(1)}, f32[1,24,768]{2,1,0:T(8,128)S(1)}, u32[]{:S(2)}, u32[]{:S(2)}) collective-permute-start(f32[1,24,768]{2,1,0:T(8,128)S(1)} %get-tuple-element.31), channel_id=1, source_target_pairs={{1,0},{2,1},{3,2},{4,3},{5,4},{6,5},{7,6},{8,7},{9,8},{10,9},{11,1... | collective-permute-start | bytes 221192 | tf_op jit(solution)/shard_map/ppermute | solution.py:28
  10.9 45.1 %all-to-all-start = ((f32[12,1,512]{2,1,0:T(1,128)}), f32[12,1,512]{2,1,0:T(1,128)S(1)}, u32[]{:S(2)}, u32[]{:S(2)}) async-start(f32[12,1,512]{2,1,0:T(1,128)} %all_to_all.42), calls=%async_computation | async-start | bytes 49152 | tf_op jit(solution)/shard_map/all_to_all | solution.py:123
  46.3 30.6 %collective-permute-start.10 = (f32[6,1,64]{2,1,0:T(1,128)S(1)}, f32[6,1,64]{2,1,0:T(1,128)S(1)}, u32[]{:S(2)}, u32[]{:S(2)}) collective-permute-start(f32[6,1,64]{2,1,0:T(1,128)S(1)} %get-tuple-element.36), channel_id=1, source_target_pairs={{64,0},{128,64},{192,128},{256,192},{320,256},{384,320},{448,384},... | collective-permute-start | bytes 4616 | tf_op jit(solution)/shard_map/ppermute | solution.py:28
  47.6 29.3 %collective-permute-start.11 = (f32[6,1,64]{2,1,0:T(1,128)S(1)}, f32[6,1,64]{2,1,0:T(1,128)S(1)}, u32[]{:S(2)}, u32[]{:S(2)}) collective-permute-start(f32[6,1,64]{2,1,0:T(1,128)S(1)} %get-tuple-element.37), channel_id=1, source_target_pairs={{0,64},{64,128},{128,192},{192,256},{256,320},{320,384},{384,448},... | collective-permute-start | bytes 4616 | tf_op jit(solution)/shard_map/ppermute | solution.py:26
  56.1 20.7 %all-to-all-start.1 = ((f32[12,1,512]{2,1,0:T(1,128)}), f32[12,1,512]{2,1,0:T(1,128)S(1)}, u32[]{:S(2)}, u32[]{:S(2)}) async-start(f32[12,1,512]{2,1,0:T(1,128)} %all_to_all.43), calls=%async_computation.1 | async-start | bytes 49152 | tf_op jit(solution)/shard_map/all_to_all | solution.py:122
  80.8 21.8 %collective-permute-start.16 = (f32[1,24,64]{2,1,0:T(8,128)S(1)}, f32[1,24,64]{2,1,0:T(8,128)S(1)}, u32[]{:S(2)}, u32[]{:S(2)}) collective-permute-start(f32[1,24,64]{2,1,0:T(8,128)S(1)} %get-tuple-element.45), channel_id=1, source_target_pairs={{0,1},{1,2},{2,3},{3,4},{4,5},{5,6},{6,7},{7,8},{8,9},{9,10},{10,1... | collective-permute-start | bytes 18440 | tf_op jit(solution)/shard_map/ppermute | solution.py:26
  82.7 19.8 %collective-permute-start.17 = (f32[1,24,64]{2,1,0:T(8,128)S(1)}, f32[1,24,64]{2,1,0:T(8,128)S(1)}, u32[]{:S(2)}, u32[]{:S(2)}) collective-permute-start(f32[1,24,64]{2,1,0:T(8,128)S(1)} %get-tuple-element.44), channel_id=1, source_target_pairs={{1,0},{2,1},{3,2},{4,3},{5,4},{6,5},{7,6},{8,7},{9,8},{10,9},{11,1... | collective-permute-start | bytes 18440 | tf_op jit(solution)/shard_map/ppermute | solution.py:28
  88.5 40.2 %all-to-all-start.2 = ((f32[12,1,512]{2,1,0:T(1,128)}), f32[12,1,512]{2,1,0:T(1,128)}, u32[]{:S(2)}, u32[]{:S(2)}) async-start(f32[12,1,512]{2,1,0:T(1,128)} %mul.975), calls=%async_computation.2 | async-start | bytes 49152 | tf_op jit(solution)/shard_map/all_to_all | solution.py:123
  93.4 20.7 %collective-permute-start.2 = (f32[6,1,768]{2,1,0:T(1,128)S(1)}, f32[6,1,768]{2,1,0:T(1,128)S(1)}, u32[]{:S(2)}, u32[]{:S(2)}) collective-permute-start(f32[6,1,768]{2,1,0:T(1,128)S(1)} %get-tuple-element.24), channel_id=1, source_target_pairs={{0,64},{64,128},{128,192},{192,256},{256,320},{320,384},{384,448},... | collective-permute-start | bytes 55304 | tf_op jit(solution)/shard_map/ppermute | solution.py:26
  103.2 45.8 %collective-permute-start.18 = (f32[6,1,64]{2,1,0:T(1,128)}, f32[6,1,64]{2,1,0:T(1,128)}, u32[]{:S(2)}, u32[]{:S(2)}) collective-permute-start(f32[6,1,64]{2,1,0:T(1,128)} %get-tuple-element.34), channel_id=1, source_target_pairs={{64,0},{128,64},{192,128},{256,192},{320,256},{384,320},{448,384},... | collective-permute-start | bytes 4616 | tf_op jit(solution)/shard_map/ppermute | solution.py:28
  104.4 44.5 %collective-permute-start.19 = (f32[6,1,64]{2,1,0:T(1,128)}, f32[6,1,64]{2,1,0:T(1,128)}, u32[]{:S(2)}, u32[]{:S(2)}) collective-permute-start(f32[6,1,64]{2,1,0:T(1,128)} %get-tuple-element.35), channel_id=1, source_target_pairs={{0,64},{64,128},{128,192},{192,256},{256,320},{320,384},{384,448},... | collective-permute-start | bytes 4616 | tf_op jit(solution)/shard_map/ppermute | solution.py:26
  121.0 43.1 %collective-permute-start.4 = (f32[1,24,768]{2,1,0:T(8,128)S(1)}, f32[1,24,768]{2,1,0:T(8,128)S(1)}, u32[]{:S(2)}, u32[]{:S(2)}) collective-permute-start(f32[1,24,768]{2,1,0:T(8,128)S(1)} %get-tuple-element.28), channel_id=1, source_target_pairs={{0,1},{1,2},{2,3},{3,4},{4,5},{5,6},{6,7},{7,8},{8,9},{9,10},{10,1... | collective-permute-start | bytes 221192 | tf_op jit(solution)/shard_map/ppermute | solution.py:26
  122.9 41.2 %collective-permute-start.5 = (f32[1,24,768]{2,1,0:T(8,128)S(1)}, f32[1,24,768]{2,1,0:T(8,128)S(1)}, u32[]{:S(2)}, u32[]{:S(2)}) collective-permute-start(f32[1,24,768]{2,1,0:T(8,128)S(1)} %get-tuple-element.29), channel_id=1, source_target_pairs={{1,0},{2,1},{3,2},{4,3},{5,4},{6,5},{7,6},{8,7},{9,8},{10,9},{11,1... | collective-permute-start | bytes 221192 | tf_op jit(solution)/shard_map/ppermute | solution.py:28
  128.7 20.2 %all-to-all-start.3 = ((f32[12,1,512]{2,1,0:T(1,128)}), f32[12,1,512]{2,1,0:T(1,128)S(1)}, u32[]{:S(2)}, u32[]{:S(2)}) async-start(f32[12,1,512]{2,1,0:T(1,128)} %all_to_all.44), calls=%async_computation.3 | async-start | bytes 49152 | tf_op jit(solution)/shard_map/all_to_all | solution.py:122
  151.5 21.7 %collective-permute-start.20 = (f32[1,24,64]{2,1,0:T(8,128)S(1)}, f32[1,24,64]{2,1,0:T(8,128)S(1)}, u32[]{:S(2)}, u32[]{:S(2)}) collective-permute-start(f32[1,24,64]{2,1,0:T(8,128)S(1)} %get-tuple-element.39), channel_id=1, source_target_pairs={{0,1},{1,2},{2,3},{3,4},{4,5},{5,6},{6,7},{7,8},{8,9},{9,10},{10,1... | collective-permute-start | bytes 18440 | tf_op jit(solution)/shard_map/ppermute | solution.py:26
  153.4 19.8 %collective-permute-start.21 = (f32[1,24,64]{2,1,0:T(8,128)S(1)}, f32[1,24,64]{2,1,0:T(8,128)S(1)}, u32[]{:S(2)}, u32[]{:S(2)}) collective-permute-start(f32[1,24,64]{2,1,0:T(8,128)S(1)} %get-tuple-element.38), channel_id=1, source_target_pairs={{1,0},{2,1},{3,2},{4,3},{5,4},{6,5},{7,6},{8,7},{9,8},{10,9},{11,1... | collective-permute-start | bytes 18440 | tf_op jit(solution)/shard_map/ppermute | solution.py:28
  159.2 44.2 %all-to-all-start.4 = ((f32[12,1,512]{2,1,0:T(1,128)}), f32[12,1,512]{2,1,0:T(1,128)}, u32[]{:S(2)}, u32[]{:S(2)}) async-start(f32[12,1,512]{2,1,0:T(1,128)} %mul.976), calls=%async_computation.4 | async-start | bytes 49152 | tf_op jit(solution)/shard_map/all_to_all | solution.py:123
  164.2 20.7 %collective-permute-start.6 = (f32[6,1,768]{2,1,0:T(1,128)S(1)}, f32[6,1,768]{2,1,0:T(1,128)S(1)}, u32[]{:S(2)}, u32[]{:S(2)}) collective-permute-start(f32[6,1,768]{2,1,0:T(1,128)S(1)} %get-tuple-element.22), channel_id=1, source_target_pairs={{0,64},{64,128},{128,192},{192,256},{256,320},{320,384},{384,448},... | collective-permute-start | bytes 55304 | tf_op jit(solution)/shard_map/ppermute | solution.py:26
  173.9 49.9 %collective-permute-start.22 = (f32[6,1,64]{2,1,0:T(1,128)}, f32[6,1,64]{2,1,0:T(1,128)}, u32[]{:S(2)}, u32[]{:S(2)}) collective-permute-start(f32[6,1,64]{2,1,0:T(1,128)} %get-tuple-element.32), channel_id=1, source_target_pairs={{64,0},{128,64},{192,128},{256,192},{320,256},{384,320},{448,384},... | collective-permute-start | bytes 4616 | tf_op jit(solution)/shard_map/ppermute | solution.py:28
  175.1 48.6 %collective-permute-start.23 = (f32[6,1,64]{2,1,0:T(1,128)}, f32[6,1,64]{2,1,0:T(1,128)}, u32[]{:S(2)}, u32[]{:S(2)}) collective-permute-start(f32[6,1,64]{2,1,0:T(1,128)} %get-tuple-element.33), channel_id=1, source_target_pairs={{0,64},{64,128},{128,192},{192,256},{256,320},{320,384},{384,448},... | collective-permute-start | bytes 4616 | tf_op jit(solution)/shard_map/ppermute | solution.py:26
  195.8 29.7 %collective-permute-start.12 = (f32[1,24,768]{2,1,0:T(8,128)S(1)}, f32[1,24,768]{2,1,0:T(8,128)S(1)}, u32[]{:S(2)}, u32[]{:S(2)}) collective-permute-start(f32[1,24,768]{2,1,0:T(8,128)S(1)} %get-tuple-element.26), channel_id=1, source_target_pairs={{0,1},{1,2},{2,3},{3,4},{4,5},{5,6},{6,7},{7,8},{8,9},{9,10},{10,1... | collective-permute-start | bytes 221192 | tf_op jit(solution)/shard_map/ppermute | solution.py:26
  197.7 27.8 %collective-permute-start.13 = (f32[1,24,768]{2,1,0:T(8,128)S(1)}, f32[1,24,768]{2,1,0:T(8,128)S(1)}, u32[]{:S(2)}, u32[]{:S(2)}) collective-permute-start(f32[1,24,768]{2,1,0:T(8,128)S(1)} %get-tuple-element.27), channel_id=1, source_target_pairs={{1,0},{2,1},{3,2},{4,3},{5,4},{6,5},{7,6},{8,7},{9,8},{10,9},{11,1... | collective-permute-start | bytes 221192 | tf_op jit(solution)/shard_map/ppermute | solution.py:28
  203.5 20.2 %all-to-all-start.5 = ((f32[12,1,512]{2,1,0:T(1,128)}), f32[12,1,512]{2,1,0:T(1,128)S(1)}, u32[]{:S(2)}, u32[]{:S(2)}) async-start(f32[12,1,512]{2,1,0:T(1,128)} %all_to_all.45), calls=%async_computation.5 | async-start | bytes 49152 | tf_op jit(solution)/shard_map/all_to_all | solution.py:122
  (48 other events, 501.7 us)
where the time goes:
time: 250 us; the launch traced here: 248 us
  starting transfers between devices  158 us (63%)
  local copies, waits for them, and re-layouts  36.7 us (15%)
  waiting for transfers between devices  28.4 us (11%)
  other arithmetic  21.7 us (9%)
    ppermute x12, starting transfers between devices, with_halo(): lax.ppermute(tail, axis, [(i, (i + 1) % count) for i in range(ends)])  59.8 us
    ppermute x12, starting transfers between devices, with_halo(): lax.ppermute(head, axis, [((i + 1) % count, i) for i in range(ends)])  42.2 us
    all_to_all x3, starting transfers between devices, couple(): lax.all_to_all(outgoing, 'sec', split_axis=0, concat_axis=0, tiled=True)  30.5 us
    all_to_all x3, starting transfers between devices, couple(): lax.all_to_all(homeward, 'sec', split_axis=0, concat_axis=0, tiled=True)  25.2 us
    all_to_all x3, waiting for transfers between devices, couple(): lax.all_to_all(outgoing, 'sec', split_axis=0, concat_axis=0, tiled=True)  20.8 us
    mul x12, local copies, waits for them, and re-layouts, turn_grow(): aligned = zonal[..., None] * east_part + meridional[..., None] * north_part  7.72 us
    ppermute x12, waiting for transfers between devices, with_halo(): lax.ppermute(head, axis, [((i + 1) % count, i) for i in range(ends)])  7.56 us
  transfers between devices with their start and end apart: 30, of which 4 were waited for; matrix products, arithmetic and copies ran while one was open for 18% of the time, Pallas kernels for 0%

commit v1 on v0

v1 whole, which is shorter than its diff:
```python
import math

import jax
import jax.numpy as jnp
import ml_dtypes
import numpy as np
from jax import lax
from jax.experimental import pallas as pl
from jax.experimental.pallas import tpu as pltpu
from jax.sharding import PartitionSpec as P

NFREQ = 24
NDIR = 32
NDEPTH = 32
STEPS = 3
ROWS = 4
COLS = 24
CELLS = ROWS * COLS
SPEC = NFREQ * NDIR
WIDE = SPEC + 128

STOKES_SCALE = 0.1
OCEAN_DT = 0.3
CURRENT_GAIN = 0.2

MESH = pl.DeviceIdType.MESH


def halves(table):
    high = table.astype(ml_dtypes.bfloat16)
    low = (table - high.astype(np.float32)).astype(ml_dtypes.bfloat16)
    return high, low


def build_tables():
    f32 = np.float32
    fraction = np.arange(NFREQ, dtype=f32) / f32(NFREQ - 1)
    angles = (np.arange(NDIR, dtype=f32) + f32(0.5)) * f32(2.0 * math.pi / NDIR)
    east = np.cos(angles).astype(f32)
    north = np.sin(angles).astype(f32)
    compass = np.stack([east, north])
    courant = f32(0.1) + f32(0.3) * fraction
    depth_level = f32(0.5) + f32(NDEPTH - 2) * (f32(1.0) - fraction)
    levels = np.arange(NDEPTH, dtype=f32)
    weights = np.maximum(f32(1.0) - np.abs(levels[None, :] - depth_level[:, None]), f32(0.0))
    mean_weights = weights / np.sum(weights, axis=1, keepdims=True)
    x_rate = (courant[:, None] * east[None, :]).reshape(-1)
    y_rate = (courant[:, None] * north[None, :]).reshape(-1)
    turn_gain = f32(1.0) - f32(0.5) * fraction
    growth = f32(CURRENT_GAIN) * (f32(1.0) + fraction)
    stokes = (
        f32(STOKES_SCALE) * weights[:, None, None, :] * compass.T[None, :, :, None]
    ).reshape(SPEC, 2 * NDEPTH)
    swell = (
        growth[None, None, :, None] * mean_weights.T[None, :, :, None] * compass[:, None, None, :]
    ).reshape(2 * NDEPTH, SPEC)
    rates = np.zeros((8, SPEC), f32)
    rates[0] = f32(1.0) - np.abs(x_rate) - np.abs(y_rate)
    rates[1] = np.abs(x_rate)
    rates[2] = np.abs(y_rate)
    rates[3] = np.repeat(turn_gain, NDIR)
    stokes_table = np.concatenate(halves(stokes), axis=1)
    swell_high, swell_low = halves(swell)
    swell_table = np.concatenate([swell_high, swell_high, swell_low], axis=0)
    return rates, stokes_table, swell_table


def iota(shape, dim):
    return lax.broadcasted_iota(jnp.int32, shape, dim)


def round_half(x):
    return x.astype(jnp.bfloat16).astype(jnp.float32)


def kernel(
    sections,
    bands,
    spectra_hbm,
    turning_ref,
    currents_ref,
    drag_ref,
    land_ref,
    target_ref,
    rates_ref,
    stokes_hbm,
    swell_hbm,
    spectra_out,
    currents_out,
    state,
    south_halo,
    north_halo,
    west_halo,
    east_halo,
    west_edge,
    east_edge,
    outgoing,
    arrived,
    turned,
    stokes_table,
    swell_table,
    tiny,
    turn_size,
    turn_sign,
    sea,
    load_sem,
    lat_send,
    lat_recv,
    sec_send,
    sec_recv,
    pair_send,
    pair_recv,
):
    f32, bf16 = jnp.float32, jnp.bfloat16
    share = CELLS // sections
    sec = lax.axis_index("sec")
    lat = lax.axis_index("lat")
    has_west, has_east = sec > 0, sec < sections - 1
    has_south, has_north = lat > 0, lat < bands - 1

    loads = [
        pltpu.make_async_copy(spectra_hbm, state.at[0, :, pl.ds(0, SPEC)], load_sem.at[0]),
        pltpu.make_async_copy(stokes_hbm, stokes_table, load_sem.at[1]),
        pltpu.make_async_copy(swell_hbm, swell_table, load_sem.at[2]),
    ]
    for load in loads:
        load.start()

    barrier = pltpu.get_barrier_semaphore()
    for ahead in range(1, sections):
        peer = lax.rem(sec + ahead, sections)
        pl.semaphore_signal(barrier, inc=1, device_id={"sec": peer}, device_id_type=MESH)

    @pl.when(has_south)
    def _():
        pl.semaphore_signal(barrier, inc=1, device_id={"lat": lat - 1}, device_id_type=MESH)

    @pl.when(has_north)
    def _():
        pl.semaphore_signal(barrier, inc=1, device_id={"lat": lat + 1}, device_id_type=MESH)

    @pl.when(jnp.logical_not(has_south))
    def _():
        south_halo[...] = jnp.zeros_like(south_halo)

    @pl.when(jnp.logical_not(has_north))
    def _():
        north_halo[...] = jnp.zeros_like(north_halo)

    @pl.when(jnp.logical_not(has_west))
    def _():
        west_halo[...] = jnp.zeros_like(west_halo)

    @pl.when(jnp.logical_not(has_east))
    def _():
        east_halo[...] = jnp.zeros_like(east_halo)

    tiny[...] = jnp.zeros_like(tiny)
    tiny[0, 0:ROWS, 0:COLS] = turning_ref[...]
    tiny[1, 0:ROWS, 0:COLS] = land_ref[...].astype(f32)
    tiny[2, 0:ROWS, 0:COLS] = target_ref[...].astype(f32)
    tiny[3, 0:1, 0:NDEPTH] = 1.0 - drag_ref[...]
    lane_row = iota((1, 128), 1)
    target_rows = tiny[2]
    targets = jnp.full((1, 128), 99.0, f32)
    for y in range(ROWS):
        row = target_rows[y : y + 1, :]
        moved = pltpu.roll(row, COLS * y, 1) if y else row
        inside = jnp.logical_and(lane_row >= COLS * y, lane_row < COLS * (y + 1))
        targets = jnp.where(inside, moved, targets)
    matches = (iota((16, 128), 0).astype(f32) == targets).astype(f32)
    earlier = (iota((128, 128), 0) < iota((128, 128), 1)).astype(f32)
    before = jnp.dot(matches.astype(bf16), earlier.astype(bf16), preferred_element_type=f32)
    rank = jnp.sum(matches * before, axis=0, keepdims=True)
    place_of = targets * share + rank
    place = (iota((128, 128), 0).astype(f32) == place_of).astype(f32)
    place_back = jnp.transpose(place)[0:CELLS, 0:CELLS].astype(bf16)
    place = place[0:CELLS, 0:CELLS].astype(bf16)

    turn_columns = jnp.transpose(tiny[0])
    sea_columns = jnp.transpose(tiny[1])
    for y in range(ROWS):
        rows = slice(COLS * y, COLS * (y + 1))
        turn = jnp.broadcast_to(turn_columns[0:COLS, y : y + 1], (COLS, 128))
        turn_size[rows, :] = jnp.abs(turn)
        turn_sign[rows, :] = turn
        sea[rows, :] = jnp.broadcast_to(sea_columns[0:COLS, y : y + 1], (COLS, 128))

    keep = tiny[3, 0:1, :]
    keep = keep + pltpu.roll(keep, 32, 1)
    keep = keep + pltpu.roll(keep, 64, 1)

    lane = iota((COLS, 128), 1)
    line = iota((COLS, 128), 0)
    first_column = line == 0
    last_column = line == COLS - 1
    direction = lane & (NDIR - 1)
    goes_east = jnp.logical_or(direction < NDIR // 4, direction >= 3 * NDIR // 4)
    goes_north = direction < NDIR // 2
    first_direction = direction == 0
    last_direction = direction == NDIR - 1
    zonal = (lane & 63) < 32
    low_half = iota((CELLS, 128), 1) < 64
    twist = jnp.where(zonal, OCEAN_DT, -OCEAN_DT)

    def edge_rows(step):
        for y in range(ROWS):
            west_edge[step, y : y + 1, :] = state[step, COLS * y : COLS * y + 1, :]
            east_edge[step, y : y + 1, :] = state[step, COLS * (y + 1) - 1 : COLS * (y + 1), :]

    def to_south(step):
        return pltpu.make_async_remote_copy(
            src_ref=state.at[step, pl.ds(0, COLS)],
            dst_ref=north_halo.at[step],
            send_sem=lat_send.at[step, 0],
            recv_sem=lat_recv.at[step, 0],
            device_id={"lat": lat - 1},
            device_id_type=MESH,
        )

    def to_north(step):
        return pltpu.make_async_remote_copy(
            src_ref=state.at[step, pl.ds(CELLS - COLS, COLS)],
            dst_ref=south_halo.at[step],
            send_sem=lat_send.at[step, 1],
            recv_sem=lat_recv.at[step, 1],
            device_id={"lat": lat + 1},
            device_id_type=MESH,
        )

    def to_west(step):
        return pltpu.make_async_remote_copy(
            src_ref=west_edge.at[step],
            dst_ref=east_halo.at[step],
            send_sem=sec_send.at[step, 0],
            recv_sem=sec_recv.at[step, 0],
            device_id={"sec": sec - 1},
            device_id_type=MESH,
        )

    def to_east(step):
        return pltpu.make_async_remote_copy(
            src_ref=east_edge.at[step],
            dst_ref=west_halo.at[step],
            send_sem=sec_send.at[step, 1],
            recv_sem=sec_recv.at[step, 1],
            device_id={"sec": sec + 1},
            device_id_type=MESH,
        )

    def each_halo(step, act):
        for there, copy in ((has_west, to_west), (has_east, to_east), (has_south, to_south), (has_north, to_north)):

            @pl.when(there)
            def _():
                act(copy(step))

    def receive_halos(step):
        for there, copy in ((has_east, to_west), (has_west, to_east), (has_north, to_south), (has_south, to_north)):

            @pl.when(there)
            def _():
                copy(step).wait_recv()

    def pair_copy(step, ahead, source):
        peer = lax.rem(sec + ahead, sections)
        slot = lax.rem(sec + sections - ahead, sections) if source else sec
        return pltpu.make_async_remote_copy(
            src_ref=outgoing.at[step, peer],
            dst_ref=arrived.at[step, slot],
            send_sem=pair_send.at[step, ahead],
            recv_sem=pair_recv.at[step, slot],
            device_id={"sec": peer},
            device_id_type=MESH,
        )

    def stokes_part(values, chunk):
        high = values.astype(bf16)
        low = (values - high.astype(f32)).astype(bf16)
        both = jnp.concatenate([high, low], axis=0)
        return jnp.dot(both, stokes_table[256 * chunk : 256 * (chunk + 1), :], preferred_element_type=f32)

    def pack(step, drift):
        drift = drift[0:CELLS] + drift[CELLS:]
        drift = drift + pltpu.roll(drift, 64, 1)
        high = round_half(drift)
        pieces = jnp.where(low_half, high, drift - high).astype(bf16)
        drift = jnp.dot(place, pieces, preferred_element_type=f32)
        drift = drift + pltpu.roll(drift, 64, 1)
        message = jnp.where(low_half, drift, state[step, :, SPEC:WIDE])
        outgoing[step] = message.reshape(sections, share, 128)

    def send_pairs(step):
        for ahead in range(1, sections):
            pair_copy(step, ahead, False).start()
        arrived[step, sec] = outgoing[step, sec]

    flows = currents_ref[...].reshape(CELLS, 2 * NDEPTH)
    state[0, :, SPEC:WIDE] = jnp.concatenate([flows, flows], axis=1)
    loads[0].wait()
    edge_rows(0)
    loads[1].wait()
    drift = stokes_part(state[0, :, 0:256], 0)
    for chunk in (1, 2):
        drift = drift + stokes_part(state[0, :, 256 * chunk : 256 * (chunk + 1)], chunk)
    pack(0, drift)
    loads[2].wait()

    greeted = sections - 1 + has_south.astype(jnp.int32) + has_north.astype(jnp.int32)
    pl.semaphore_wait(barrier, greeted)
    send_pairs(0)
    each_halo(0, lambda copy: copy.start())

    global_row = (lat * ROWS).astype(f32)

    for step in range(STEPS):
        last = step == STEPS - 1
        receive_halos(step)

        for chunk in range(SPEC // 128):
            lanes = slice(128 * chunk, 128 * (chunk + 1))
            stay = rates_ref[0:1, lanes]
            rate_x = rates_ref[1:2, lanes]
            rate_y = rates_ref[2:3, lanes]
            gain = rates_ref[3:4, lanes]
            for y in range(ROWS):
                rows = slice(COLS * y, COLS * (y + 1))
                here = state[step, rows, lanes]
                west = jnp.where(first_column, west_halo[step, y : y + 1, lanes], pltpu.roll(here, 1, 0))
                east = jnp.where(last_column, east_halo[step, y : y + 1, lanes], pltpu.roll(here, COLS - 1, 0))
                south = state[step, COLS * (y - 1) : COLS * y, lanes] if y else south_halo[step, :, lanes]
                north = (
                    state[step, COLS * (y + 1) : COLS * (y + 2), lanes]
                    if y < ROWS - 1
                    else north_halo[step, :, lanes]
                )
                moved = (
                    stay * here
                    + rate_x * jnp.where(goes_east, west, east)
                    + rate_y * jnp.where(goes_north, south, north)
                )
                behind = jnp.where(first_direction, pltpu.roll(moved, 97, 1), pltpu.roll(moved, 1, 1))
                forward = jnp.where(last_direction, pltpu.roll(moved, 31, 1), pltpu.roll(moved, 127, 1))
                beside = jnp.where(turn_sign[rows, :] > 0.0, behind, forward)
                rate = turn_size[rows, :] * gain
                turned[rows, lanes] = (moved + rate * (beside - moved)) * sea[rows, :]

        for ahead in range(1, sections):
            pair_copy(step, ahead, True).wait_recv()

        message = arrived[step].reshape(CELLS, 128)
        high = round_half(message)
        pieces = jnp.where(low_half, pltpu.roll(high, 64, 1), message - high).astype(bf16)
        seen = jnp.dot(place_back, pieces, preferred_element_type=f32).astype(bf16)
        seen = jnp.concatenate([seen, seen[:, 0:64]], axis=1)
        drift = None
        for chunk in range(SPEC // 256):
            lanes = slice(256 * chunk, 256 * (chunk + 1))
            grow = jnp.dot(seen, swell_table[:, lanes], preferred_element_type=f32)
            waves = turned[:, lanes] * (1.0 + grow)
            if last:
                spectra_out[:, lanes] = waves
            else:
                state[step + 1, :, lanes] = waves
                part = stokes_part(waves, chunk)
                drift = part if drift is None else drift + part

        drag = jnp.where(low_half, message, pltpu.roll(message, 64, 1))
        for y in range(ROWS):
            rows = slice(COLS * y, COLS * (y + 1))
            lanes = slice(SPEC, WIDE)
            here = state[step, rows, lanes]
            west = jnp.where(first_column, west_halo[step, y : y + 1, lanes], pltpu.roll(here, 1, 0))
            east = jnp.where(last_column, east_halo[step, y : y + 1, lanes], pltpu.roll(here, COLS - 1, 0))
            south = state[step, COLS * (y - 1) : COLS * y, lanes] if y else south_halo[step, :, lanes]
            north = (
                state[step, COLS * (y + 1) : COLS * (y + 2), lanes] if y < ROWS - 1 else north_halo[step, :, lanes]
            )
            sheared = jnp.where(zonal, south - north, east - west)
            spin = 0.5 * (sheared + pltpu.roll(sheared, 32, 1))
            spin = spin + (0.2 + 0.6 * (global_row + y) / (ROWS * bands))
            pushed = pltpu.roll(here + drag[rows, :], 32, 1)
            flow = (keep * sea[rows, :]) * (here + twist * spin * pushed)
            if last:
                currents_out[rows, :] = flow[:, 0 : 2 * NDEPTH]
            else:
                state[step + 1, rows, lanes] = flow

        if not last:
            edge_rows(step + 1)
            each_halo(step + 1, lambda copy: copy.start())
            pack(step + 1, drift)
            send_pairs(step + 1)

    for step in range(STEPS):
        each_halo(step, lambda copy: copy.wait_send())
        for ahead in range(1, sections):
            pair_copy(step, ahead, False).wait_send()


def solution(mesh):
    sections, bands = mesh.shape["sec"], mesh.shape["lat"]
    rates, stokes_table, swell_table = build_tables()
    share = CELLS // sections

    def per_device(spectra, turning, currents, drag_rates, land_mask, ocean_target):
        f32, bf16 = jnp.float32, jnp.bfloat16
        vmem = pl.BlockSpec(memory_space=pltpu.VMEM)
        hbm = pl.BlockSpec(memory_space=pltpu.HBM)
        waves, flows = pl.pallas_call(
            lambda *refs: kernel(sections, bands, *refs),
            out_shape=(
                jax.ShapeDtypeStruct((CELLS, SPEC), f32),
                jax.ShapeDtypeStruct((CELLS, 2 * NDEPTH), f32),
            ),
            in_specs=[hbm, vmem, vmem, vmem, vmem, vmem, vmem, hbm, hbm],
            out_specs=(vmem, vmem),
            scratch_shapes=[
                pltpu.VMEM((STEPS, CELLS, WIDE), f32),
                pltpu.VMEM((STEPS, COLS, WIDE), f32),
                pltpu.VMEM((STEPS, COLS, WIDE), f32),
                pltpu.VMEM((STEPS, ROWS, WIDE), f32),
                pltpu.VMEM((STEPS, ROWS, WIDE), f32),
                pltpu.VMEM((STEPS, ROWS, WIDE), f32),
                pltpu.VMEM((STEPS, ROWS, WIDE), f32),
                pltpu.VMEM((STEPS, sections, share, 128), f32),
                pltpu.VMEM((STEPS, sections, share, 128), f32),
                pltpu.VMEM((CELLS, SPEC), f32),
                pltpu.VMEM((SPEC, 128), bf16),
                pltpu.VMEM((6 * NDEPTH, SPEC), bf16),
                pltpu.VMEM((4, 8, 128), f32),
                pltpu.VMEM((CELLS, 128), f32),
                pltpu.VMEM((CELLS, 128), f32),
                pltpu.VMEM((CELLS, 128), f32),
                pltpu.SemaphoreType.DMA((3,)),
                pltpu.SemaphoreType.DMA((STEPS, 2)),
                pltpu.SemaphoreType.DMA((STEPS, 2)),
                pltpu.SemaphoreType.DMA((STEPS, 2)),
                pltpu.SemaphoreType.DMA((STEPS, 2)),
                pltpu.SemaphoreType.DMA((STEPS, sections)),
                pltpu.SemaphoreType.DMA((STEPS, sections)),
            ],
            compiler_params=pltpu.CompilerParams(
                collective_id=0, has_side_effects=True, vmem_limit_bytes=24 << 20
            ),
        )(
            spectra.reshape(CELLS, SPEC),
            turning,
            currents,
            drag_rates.reshape(1, NDEPTH),
            land_mask,
            ocean_target,
            jnp.asarray(rates),
            jnp.asarray(stokes_table),
            jnp.asarray(swell_table),
        )
        return waves.reshape(ROWS, COLS, SPEC), flows.reshape(ROWS, COLS, 2 * NDEPTH)

    return jax.shard_map(
        per_device,
        mesh=mesh,
        in_specs=(
            P("lat", "sec", None),
            P("lat", "sec"),
            P("lat", "sec", None),
            P(),
            P("lat", "sec"),
            P("lat", "sec"),
        ),
        out_specs=(P("lat", "sec", None), P("lat", "sec", None)),
        check_vma=False,
    )
```

time: 250 us -> 48.2 us (0.19)
  starting transfers between devices: 158 us -> 0 us
  Pallas kernels: 0 us -> 39.3 us
  local copies, waits for them, and re-layouts: 36.7 us -> 7.75 us
  waiting for transfers between devices: 28.4 us -> 0 us
  other arithmetic: 21.7 us -> 0 us
    ppermute x24 -> x0, starting transfers between devices: 102 us -> none  [the longest x12 59.8 us: with_halo(): lax.ppermute(tail, axis, [(i, (i + 1) % count) for i in range(ends)])]
    all_to_all x6 -> x0, starting transfers between devices: 55.7 us -> none  [the longest x3 30.5 us: couple(): lax.all_to_all(outgoing, 'sec', split_axis=0, concat_axis=0, tiled=True)]
    pallas_call x0 -> x1, Pallas kernels: none -> 39.3 us  [per_device(): pl.pallas_call(lambda *refs: kernel(sections, bands, *refs), out_shape=(j...]
    all_to_all x6 -> x0, waiting for transfers between devices: 20.8 us -> none  [the longest x3 20.8 us: couple(): lax.all_to_all(outgoing, 'sec', split_axis=0, concat_axis=0, tiled=True)]
    mul x28 -> x0, local copies, waits for them, and re-layouts: 11.8 us -> none  [the longest x12 7.72 us: turn_grow(): aligned = zonal[..., None] * east_part + meridional[..., None] * north_part]
    mul x16 -> x0, other arithmetic: 7.93 us -> none  [the longest x3 3.21 us: per_device(): turn_grow(advected, turning, current_eff.reshape(lat_rows, lon_cols, -1),...]
    ppermute x24 -> x0, waiting for transfers between devices: 7.59 us -> none  [the longest x12 7.56 us: with_halo(): lax.ppermute(head, axis, [((i + 1) % count, i) for i in range(ends)])]
    slice x17 -> x0, local copies, waits for them, and re-layouts: 6.33 us -> none  [the longest x6 4.36 us: turn_grow(): behind = jnp.roll(spread, 1, axis=-1)]
  transfers between devices with their start and end apart: 30 -> 0, of which waited for: 4 -> 0; matrix products, arithmetic and copies ran while one was open for 18% -> 0% of each run, Pallas kernels for 0% -> 0%
where the time goes in v1:
time: 48.2 us; the launch traced here: 47.7 us
  Pallas kernels  39.3 us (82%)
  local copies, waits for them, and re-layouts  7.75 us (16%)
  between operations  0.66 us (1%)
    pallas_call x1, Pallas kernels, per_device(): pl.pallas_call(lambda *refs: kernel(sections, bands, *refs), out_shape=(j...  39.3 us
    unnamed x20, local copies, waits for them, and re-layouts  7.75 us

profile of v1, /device:TPU:64, one launch (start us, length us, event | category | flops | bytes accessed | tf_op | source)
XLA Modules:
  0.0 47.7 jit_solution(11192505738785687295)
XLA Ops:
  0.6 0.0 copy-start.5
  0.6 0.0 copy-start.8
  0.7 0.7 %copy-done.5 = f32[4,24]{1,0:T(4,128)S(1)} copy-done((f32[4,24]{1,0:T(4,128)S(1)}, f32[4,24]{1,0:T(4,128)}, u32[]{:S(2)}) %copy-start.5) | copy-done | bytes 408
  1.3 0.0 copy-done.8
  1.3 0.0 copy-start
  1.3 1.0 %copy-done = f32[4,24,768]{2,1,0:T(8,128)S(1)} copy-done((f32[4,24,768]{2,1,0:T(8,128)S(1)}, f32[4,24,768]{2,1,0:T(8,128)}, u32[]{:S(2)}) %copy-start) | copy-done | bytes 294936
  2.3 0.0 copy-start.1
  2.3 1.0 %copy-done.1 = bf16[192,768]{1,0:T(8,128)(2,1)S(1)} copy-done((bf16[192,768]{1,0:T(8,128)(2,1)S(1)}, bf16[192,768]{1,0:T(8,128)(2,1)}, u32[]{:S(2)}) %copy-start.1) | copy-done | bytes 294936
  3.2 0.0 copy-start.2
  3.2 0.9 %copy-done.2 = bf16[768,128]{1,0:T(8,128)(2,1)S(1)} copy-done((bf16[768,128]{1,0:T(8,128)(2,1)S(1)}, bf16[768,128]{1,0:T(8,128)(2,1)}, u32[]{:S(2)}) %copy-start.2) | copy-done | bytes 196632
  4.2 0.0 copy-start.3
  4.2 0.8 %copy-done.3 = f32[4,24,64]{2,1,0:T(8,128)S(1)} copy-done((f32[4,24,64]{2,1,0:T(8,128)S(1)}, f32[4,24,64]{2,1,0:T(8,128)}, u32[]{:S(2)}) %copy-start.3) | copy-done | bytes 24600
  5.0 0.0 copy-start.4
  5.0 0.7 %copy-done.4 = f32[8,768]{1,0:T(8,128)S(1)} copy-done((f32[8,768]{1,0:T(8,128)S(1)}, f32[8,768]{1,0:T(8,128)}, u32[]{:S(2)}) %copy-start.4) | copy-done | bytes 24600
  5.7 0.0 copy-start.6
  5.7 0.7 %copy-done.6 = s32[4,24]{1,0:T(4,128)S(1)} copy-done((s32[4,24]{1,0:T(4,128)S(1)}, s32[4,24]{1,0:T(4,128)}, u32[]{:S(2)}) %copy-start.6) | copy-done | bytes 408
  6.4 0.0 copy-start.7
  6.4 0.7 %copy-done.7 = s32[4,24]{1,0:T(4,128)S(1)} copy-done((s32[4,24]{1,0:T(4,128)S(1)}, s32[4,24]{1,0:T(4,128)}, u32[]{:S(2)}) %copy-start.7) | copy-done | bytes 408
  7.1 39.3 %shard_map.104 = (f32[96,768]{1,0:T(8,128)S(1)}, f32[96,64]{1,0:T(8,128)S(1)}) custom-call(f32[96,768]{1,0:T(8,128)S(1)} %bitcast.4, f32[4,24]{1,0:T(4,128)S(1)} %copy-done.5, f32[4,24,64]{2,1,0:T(8,128)S(1)} %copy-done.3, f32[1,32]{1,0:T(1,128)S(1)} %bitcast.7, s32[4,24]{1,0:T(4,128)S(1)} %copy-done.6, s32[4,24]{1,0:T(4,128)S(1)} %copy-done.7, ...), custom_call_target="tpu_custom_call" | custom-call | tf_op jit(solution)/shard_map/pallas_call | solution.py:410
  46.4 0.7 %copy.13 = f32[4,24,768]{2,1,0:T(8,128)} copy(f32[4,24,768]{2,1,0:T(8,128)S(1)} %bitcast.5) | data formatting | bytes 589824
  47.1 0.6 %copy.14 = f32[4,24,64]{2,1,0:T(8,128)} copy(f32[4,24,64]{2,1,0:T(8,128)S(1)} %bitcast.6) | data formatting | bytes 49152
Async XLA Ops:
  0.6 0.7 %copy-start.5 = (f32[4,24]{1,0:T(4,128)S(1)}, f32[4,24]{1,0:T(4,128)}, u32[]{:S(2)}) copy-start(f32[4,24]{1,0:T(4,128)} %refs_1_.1) | copy-start | bytes 1156
  0.6 0.7 %copy-start.8 = (f32[32]{0:T(128)S(1)}, f32[32]{0:T(128)}, u32[]{:S(2)}) copy-start(f32[32]{0:T(128)} %param.12) | copy-start | bytes 388
  1.3 1.0 %copy-start = (f32[4,24,768]{2,1,0:T(8,128)S(1)}, f32[4,24,768]{2,1,0:T(8,128)}, u32[]{:S(2)}) copy-start(f32[4,24,768]{2,1,0:T(8,128)} %param.9) | copy-start | bytes 884740
  2.3 1.0 %copy-start.1 = (bf16[192,768]{1,0:T(8,128)(2,1)S(1)}, bf16[192,768]{1,0:T(8,128)(2,1)}, u32[]{:S(2)}) copy-start(bf16[192,768]{1,0:T(8,128)(2,1)} %constant.8.clone.refs_8_) | copy-start | bytes 884740
  3.2 0.9 %copy-start.2 = (bf16[768,128]{1,0:T(8,128)(2,1)S(1)}, bf16[768,128]{1,0:T(8,128)(2,1)}, u32[]{:S(2)}) copy-start(bf16[768,128]{1,0:T(8,128)(2,1)} %constant.7.clone.refs_7_) | copy-start | bytes 589828
  4.2 0.8 %copy-start.3 = (f32[4,24,64]{2,1,0:T(8,128)S(1)}, f32[4,24,64]{2,1,0:T(8,128)}, u32[]{:S(2)}) copy-start(f32[4,24,64]{2,1,0:T(8,128)} %refs_2_.1) | copy-start | bytes 73732
  5.0 0.7 %copy-start.4 = (f32[8,768]{1,0:T(8,128)S(1)}, f32[8,768]{1,0:T(8,128)}, u32[]{:S(2)}) copy-start(f32[8,768]{1,0:T(8,128)} %constant.6.clone.refs_6_) | copy-start | bytes 73732
  5.7 0.7 %copy-start.6 = (s32[4,24]{1,0:T(4,128)S(1)}, s32[4,24]{1,0:T(4,128)}, u32[]{:S(2)}) copy-start(s32[4,24]{1,0:T(4,128)} %refs_4_.1) | copy-start | bytes 1156
  6.4 0.7 %copy-start.7 = (s32[4,24]{1,0:T(4,128)S(1)}, s32[4,24]{1,0:T(4,128)}, u32[]{:S(2)}) copy-start(s32[4,24]{1,0:T(4,128)} %refs_5_.1) | copy-start | bytes 1156

commit v2 on v1

v2 whole, which is shorter than its diff:
```python
import math

import jax
import jax.numpy as jnp
import ml_dtypes
import numpy as np
from jax import lax
from jax.experimental import pallas as pl
from jax.experimental.pallas import tpu as pltpu
from jax.sharding import PartitionSpec as P

NFREQ = 24
NDIR = 32
NDEPTH = 32
STEPS = 3
ROWS = 4
COLS = 24
CELLS = ROWS * COLS
SPEC = NFREQ * NDIR
WIDE = SPEC + 128

STOKES_SCALE = 0.1
OCEAN_DT = 0.3
CURRENT_GAIN = 0.2

MESH = pl.DeviceIdType.MESH


def halves(table):
    high = table.astype(ml_dtypes.bfloat16)
    low = (table - high.astype(np.float32)).astype(ml_dtypes.bfloat16)
    return high, low


def build_tables():
    f32 = np.float32
    fraction = np.arange(NFREQ, dtype=f32) / f32(NFREQ - 1)
    angles = (np.arange(NDIR, dtype=f32) + f32(0.5)) * f32(2.0 * math.pi / NDIR)
    east = np.cos(angles).astype(f32)
    north = np.sin(angles).astype(f32)
    compass = np.stack([east, north])
    courant = f32(0.1) + f32(0.3) * fraction
    depth_level = f32(0.5) + f32(NDEPTH - 2) * (f32(1.0) - fraction)
    levels = np.arange(NDEPTH, dtype=f32)
    weights = np.maximum(f32(1.0) - np.abs(levels[None, :] - depth_level[:, None]), f32(0.0))
    mean_weights = weights / np.sum(weights, axis=1, keepdims=True)
    x_rate = (courant[:, None] * east[None, :]).reshape(-1)
    y_rate = (courant[:, None] * north[None, :]).reshape(-1)
    turn_gain = f32(1.0) - f32(0.5) * fraction
    growth = f32(CURRENT_GAIN) * (f32(1.0) + fraction)
    stokes = (
        f32(STOKES_SCALE) * weights[:, None, None, :] * compass.T[None, :, :, None]
    ).reshape(SPEC, 2 * NDEPTH)
    swell = (
        growth[None, None, :, None] * mean_weights.T[None, :, :, None] * compass[:, None, None, :]
    ).reshape(2 * NDEPTH, SPEC)
    rates = np.zeros((8, SPEC), f32)
    rates[0] = f32(1.0) - np.abs(x_rate) - np.abs(y_rate)
    rates[1] = np.abs(x_rate)
    rates[2] = np.abs(y_rate)
    rates[3] = np.repeat(turn_gain, NDIR)
    stokes_table = np.concatenate(halves(stokes), axis=1)
    swell_high, swell_low = halves(swell)
    swell_table = np.concatenate([swell_high, swell_high, swell_low], axis=0)
    return rates, stokes_table, swell_table


def iota(shape, dim):
    return lax.broadcasted_iota(jnp.int32, shape, dim)


def round_half(x):
    return x.astype(jnp.bfloat16).astype(jnp.float32)


def kernel(
    sections,
    bands,
    spectra_hbm,
    turning_hbm,
    currents_hbm,
    drag_hbm,
    land_hbm,
    target_hbm,
    rates_hbm,
    stokes_hbm,
    swell_hbm,
    spectra_out,
    currents_out,
    waves,
    flows,
    wave_south,
    wave_north,
    wave_west,
    wave_east,
    flow_south,
    flow_north,
    flow_west,
    flow_east,
    wave_edges,
    flow_edges,
    outgoing,
    arrived,
    turned,
    spins,
    drifts,
    flow_at_waves,
    turning_ref,
    currents_ref,
    drag_ref,
    land_ref,
    target_ref,
    rates_ref,
    stokes_table,
    swell_table,
    tiny,
    turn_size,
    turn_sign,
    sea,
    load_sem,
    halo_send,
    halo_recv,
    pair_send,
    pair_recv,
):
    f32, bf16 = jnp.float32, jnp.bfloat16
    share = CELLS // sections
    sec = lax.axis_index("sec")
    lat = lax.axis_index("lat")
    has_west, has_east = sec > 0, sec < sections - 1
    has_south, has_north = lat > 0, lat < bands - 1

    barrier = pltpu.get_barrier_semaphore()
    for ahead in range(1, sections):
        peer = lax.rem(sec + ahead, sections)
        pl.semaphore_signal(barrier, inc=1, device_id={"sec": peer}, device_id_type=MESH)

    @pl.when(has_south)
    def _():
        pl.semaphore_signal(barrier, inc=1, device_id={"lat": lat - 1}, device_id_type=MESH)

    @pl.when(has_north)
    def _():
        pl.semaphore_signal(barrier, inc=1, device_id={"lat": lat + 1}, device_id_type=MESH)

    pairs = (
        (turning_hbm, turning_ref),
        (drag_hbm, drag_ref),
        (land_hbm, land_ref),
        (target_hbm, target_ref),
        (currents_hbm, currents_ref),
        (rates_hbm, rates_ref),
        (spectra_hbm, waves.at[0]),
        (stokes_hbm, stokes_table),
        (swell_hbm, swell_table),
    )
    loads = [pltpu.make_async_copy(there, here, load_sem.at[i]) for i, (there, here) in enumerate(pairs)]
    for load in loads:
        load.start()

    for there, halos in (
        (has_south, (wave_south, flow_south)),
        (has_north, (wave_north, flow_north)),
        (has_west, (wave_west, flow_west)),
        (has_east, (wave_east, flow_east)),
    ):

        @pl.when(jnp.logical_not(there))
        def _():
            for halo in halos:
                halo[...] = jnp.zeros_like(halo)

    tiny[...] = jnp.zeros_like(tiny)
    for load in loads[:4]:
        load.wait()
    tiny[0, 0:ROWS, 0:COLS] = turning_ref[...]
    tiny[1, 0:ROWS, 0:COLS] = land_ref[...].astype(f32)
    tiny[2, 0:ROWS, 0:COLS] = target_ref[...].astype(f32)
    tiny[3, 0:1, 0:NDEPTH] = 1.0 - drag_ref[...]

    lane_row = iota((1, 128), 1)
    target_rows = tiny[2]
    targets = jnp.full((1, 128), 99.0, f32)
    for y in range(ROWS):
        row = target_rows[y : y + 1, :]
        moved = pltpu.roll(row, COLS * y, 1) if y else row
        inside = jnp.logical_and(lane_row >= COLS * y, lane_row < COLS * (y + 1))
        targets = jnp.where(inside, moved, targets)
    matches = (iota((16, 128), 0).astype(f32) == targets).astype(f32)
    earlier = (iota((128, 128), 0) < iota((128, 128), 1)).astype(f32)
    before = jnp.dot(matches.astype(bf16), earlier.astype(bf16), preferred_element_type=f32)
    rank = jnp.sum(matches * before, axis=0, keepdims=True)
    place_of = targets * share + rank
    place = (iota((128, 128), 0).astype(f32) == place_of).astype(f32)
    place_back = jnp.transpose(place)[0:CELLS, 0:CELLS].astype(bf16)
    place = place[0:CELLS, 0:CELLS].astype(bf16)

    turn_columns = jnp.transpose(tiny[0])
    sea_columns = jnp.transpose(tiny[1])
    for y in range(ROWS):
        rows = slice(COLS * y, COLS * (y + 1))
        turn = jnp.broadcast_to(turn_columns[0:COLS, y : y + 1], (COLS, 128))
        turn_size[rows, :] = jnp.abs(turn)
        turn_sign[rows, :] = turn
        sea[rows, :] = jnp.broadcast_to(sea_columns[0:COLS, y : y + 1], (COLS, 128))

    keep = tiny[3, 0:1, :]
    keep = keep + pltpu.roll(keep, 32, 1)
    keep = keep + pltpu.roll(keep, 64, 1)

    lane = iota((COLS, 128), 1)
    line = iota((COLS, 128), 0)
    first_column = line == 0
    last_column = line == COLS - 1
    direction = lane & (NDIR - 1)
    goes_east = jnp.logical_or(direction < NDIR // 4, direction >= 3 * NDIR // 4)
    goes_north = direction < NDIR // 2
    first_direction = direction == 0
    last_direction = direction == NDIR - 1
    full_lane = iota((CELLS, 128), 1)
    low_half = full_lane < 64
    zonal = (full_lane & 63) < 32
    zonal_row = (lane & 63) < 32
    twist = jnp.where(zonal, OCEAN_DT, -OCEAN_DT)
    global_row = (lat * ROWS).astype(f32)

    def halo_copies(step, is_flow):
        own = (flows if is_flow else waves).at[step]
        edges = (flow_edges if is_flow else wave_edges).at[step]
        south, north, west, east = (
            (flow_south, flow_north, flow_west, flow_east)
            if is_flow
            else (wave_south, wave_north, wave_west, wave_east)
        )
        index = 2 * step + is_flow
        plan = (
            (has_west, has_east, edges.at[0], east, {"sec": sec - 1}),
            (has_east, has_west, edges.at[1], west, {"sec": sec + 1}),
            (has_south, has_north, own.at[pl.ds(0, COLS)], north, {"lat": lat - 1}),
            (has_north, has_south, own.at[pl.ds(CELLS - COLS, COLS)], south, {"lat": lat + 1}),
        )
        for k, (sends, receives, source, halo, device) in enumerate(plan):
            copy = lambda source=source, halo=halo, device=device, k=k: pltpu.make_async_remote_copy(
                src_ref=source,
                dst_ref=halo.at[step],
                send_sem=halo_send.at[index, k],
                recv_sem=halo_recv.at[index, k],
                device_id=device,
                device_id_type=MESH,
            )
            yield sends, receives, copy

    def send_halos(step, is_flow):
        own, edges = (flows, flow_edges) if is_flow else (waves, wave_edges)
        for y in range(ROWS):
            edges[step, 0, y : y + 1, :] = own[step, COLS * y : COLS * y + 1, :]
            edges[step, 1, y : y + 1, :] = own[step, COLS * (y + 1) - 1 : COLS * (y + 1), :]
        for sends, _, copy in halo_copies(step, is_flow):

            @pl.when(sends)
            def _():
                copy().start()

    def receive_halos(step, is_flow):
        for _, receives, copy in halo_copies(step, is_flow):

            @pl.when(receives)
            def _():
                copy().wait_recv()

    def pair_copy(index, ahead, source):
        peer = lax.rem(sec + ahead, sections)
        slot = lax.rem(sec + sections - ahead, sections) if source else sec
        return pltpu.make_async_remote_copy(
            src_ref=outgoing.at[index, peer],
            dst_ref=arrived.at[index, slot],
            send_sem=pair_send.at[index, ahead],
            recv_sem=pair_recv.at[index, slot],
            device_id={"sec": peer},
            device_id_type=MESH,
        )

    def send_pairs(index, message):
        outgoing[index] = message.reshape(sections, share, 128)
        for ahead in range(1, sections):
            pair_copy(index, ahead, False).start()
        arrived[index, sec] = outgoing[index, sec]

    def receive_pairs(index):
        for ahead in range(1, sections):
            pair_copy(index, ahead, True).wait_recv()
        return arrived[index].reshape(CELLS, 128)

    def stokes_part(values, chunk):
        high = values.astype(bf16)
        low = (values - high.astype(f32)).astype(bf16)
        both = jnp.concatenate([high, low], axis=0)
        return jnp.dot(both, stokes_table[256 * chunk : 256 * (chunk + 1), :], preferred_element_type=f32)

    def sorted_drift(step, drift):
        drift = drift[0:CELLS] + drift[CELLS:]
        drift = drift + pltpu.roll(drift, 64, 1)
        drifts[step] = drift
        high = round_half(drift)
        pieces = jnp.where(low_half, high, drift - high).astype(bf16)
        drift = jnp.dot(place, pieces, preferred_element_type=f32)
        return drift + pltpu.roll(drift, 64, 1)

    def neighbours(own, halos, step, y, lanes):
        south, north, west, east = halos
        rows = slice(COLS * y, COLS * (y + 1))
        here = own[step, rows, lanes]
        return (
            here,
            jnp.where(first_column, west[step, y : y + 1, lanes], pltpu.roll(here, 1, 0)),
            jnp.where(last_column, east[step, y : y + 1, lanes], pltpu.roll(here, COLS - 1, 0)),
            own[step, COLS * (y - 1) : COLS * y, lanes] if y else south[step, :, lanes],
            own[step, COLS * (y + 1) : COLS * (y + 2), lanes] if y < ROWS - 1 else north[step, :, lanes],
        )

    def find_spin(step):
        for y in range(ROWS):
            _, west, east, south, north = neighbours(
                flows, (flow_south, flow_north, flow_west, flow_east), step, y, slice(0, 128)
            )
            sheared = jnp.where(zonal_row, south - north, east - west)
            spin = 0.5 * (sheared + pltpu.roll(sheared, 32, 1))
            spins[step, COLS * y : COLS * (y + 1), :] = spin + (0.2 + 0.6 * (global_row + y) / (ROWS * bands))

    def advect(step):
        for chunk in range(SPEC // 128):
            lanes = slice(128 * chunk, 128 * (chunk + 1))
            stay = rates_ref[0:1, lanes]
            rate_x = rates_ref[1:2, lanes]
            rate_y = rates_ref[2:3, lanes]
            gain = rates_ref[3:4, lanes]
            for y in range(ROWS):
                rows = slice(COLS * y, COLS * (y + 1))
                here, west, east, south, north = neighbours(
                    waves, (wave_south, wave_north, wave_west, wave_east), step, y, lanes
                )
                moved = (
                    stay * here
                    + rate_x * jnp.where(goes_east, west, east)
                    + rate_y * jnp.where(goes_north, south, north)
                )
                behind = jnp.where(first_direction, pltpu.roll(moved, 97, 1), pltpu.roll(moved, 1, 1))
                forward = jnp.where(last_direction, pltpu.roll(moved, 31, 1), pltpu.roll(moved, 127, 1))
                beside = jnp.where(turn_sign[rows, :] > 0.0, behind, forward)
                rate = turn_size[rows, :] * gain
                turned[rows, lanes] = (moved + rate * (beside - moved)) * sea[rows, :]

    def push(flow, spin, drift, wet):
        return (keep * wet) * (flow + twist * spin * pltpu.roll(flow + drift, 32, 1))

    def grow(seen, step):
        seen = jnp.concatenate([seen, seen[:, 0:64]], axis=1)
        drift = None
        for chunk in range(SPEC // 256):
            lanes = slice(256 * chunk, 256 * (chunk + 1))
            growth = jnp.dot(seen, swell_table[:, lanes], preferred_element_type=f32)
            values = turned[:, lanes] * (1.0 + growth)
            if step == STEPS:
                spectra_out[:, lanes] = values
            else:
                waves[step, :, lanes] = values
        if step == STEPS:
            return None
        send_halos(step, 0)
        return find_drift(step)

    def find_drift(step):
        drift = None
        for chunk in range(SPEC // 256):
            part = stokes_part(waves[step, :, 256 * chunk : 256 * (chunk + 1)], chunk)
            drift = part if drift is None else drift + part
        return sorted_drift(step, drift)

    def first_seen(message):
        high = round_half(message)
        pieces = jnp.where(low_half, pltpu.roll(high, 64, 1), message - high).astype(bf16)
        seen = jnp.dot(place_back, pieces, preferred_element_type=f32)
        flow_at_waves[0] = seen + pltpu.roll(seen, 64, 1)
        return seen.astype(bf16)

    def next_seen(step, message):
        high = round_half(message)
        pieces = jnp.where(low_half, high, message - high).astype(bf16)
        both = jnp.dot(place_back, pieces, preferred_element_type=f32)
        both = both + pltpu.roll(both, 64, 1)
        other = pltpu.roll(both, 32, 1)
        spin = jnp.where(zonal, both, other)
        wet = jnp.where(zonal, other, both)
        flow = push(flow_at_waves[step - 1], spin, drifts[step - 1], wet)
        flow_at_waves[step] = flow
        high = round_half(flow)
        return jnp.where(low_half, high, flow - high).astype(bf16)

    def spin_message(step):
        return jnp.where(zonal, spins[step], sea[...])

    loads[4].wait()
    start_flow = currents_ref[...].reshape(CELLS, 2 * NDEPTH)
    flows[0] = jnp.concatenate([start_flow, start_flow], axis=1)
    for load in loads[5:]:
        load.wait()
    drift = find_drift(0)

    greeted = sections - 1 + has_south.astype(jnp.int32) + has_north.astype(jnp.int32)
    pl.semaphore_wait(barrier, greeted)

    send_halos(0, 1)
    send_pairs(0, jnp.where(low_half, drift, flows[0]))
    send_halos(0, 0)

    receive_halos(0, 1)
    find_spin(0)
    send_pairs(1, spin_message(0))
    receive_halos(0, 0)
    advect(0)
    message = receive_pairs(0)
    flows[1] = push(flows[0], spins[0], jnp.where(low_half, message, pltpu.roll(message, 64, 1)), sea[...])
    send_halos(1, 1)
    send_pairs(2, grow(first_seen(message), 1))

    receive_halos(1, 1)
    find_spin(1)
    send_pairs(3, spin_message(1))
    receive_halos(1, 0)
    advect(1)
    send_pairs(4, grow(next_seen(1, receive_pairs(1)), 2))
    flows[2] = push(flows[1], spins[1], receive_pairs(2), sea[...])
    send_halos(2, 1)

    receive_halos(2, 0)
    advect(2)
    grow(next_seen(2, receive_pairs(3)), 3)
    receive_halos(2, 1)
    find_spin(2)
    currents_out[...] = push(flows[2], spins[2], receive_pairs(4), sea[...])[:, 0 : 2 * NDEPTH]

    for step in range(STEPS):
        for is_flow in (0, 1):
            for sends, _, copy in halo_copies(step, is_flow):

                @pl.when(sends)
                def _():
                    copy().wait_send()

    for index in range(2 * STEPS - 1):
        for ahead in range(1, sections):
            pair_copy(index, ahead, False).wait_send()


def store(waves_ref, flows_ref, waves_out, flows_out, sems):
    copies = [
        pltpu.make_async_copy(waves_ref, waves_out, sems.at[0]),
        pltpu.make_async_copy(flows_ref, flows_out, sems.at[1]),
    ]
    for copy in copies:
        copy.start()
    for copy in copies:
        copy.wait()


def solution(mesh):
    sections, bands = mesh.shape["sec"], mesh.shape["lat"]
    rates, stokes_table, swell_table = build_tables()
    share = CELLS // sections

    def per_device(spectra, turning, currents, drag_rates, land_mask, ocean_target):
        f32, bf16 = jnp.float32, jnp.bfloat16
        vmem = pl.BlockSpec(memory_space=pltpu.VMEM)
        hbm = pl.BlockSpec(memory_space=pltpu.HBM)
        operands = (
            spectra.reshape(CELLS, SPEC),
            turning,
            currents,
            drag_rates.reshape(1, NDEPTH),
            land_mask,
            ocean_target,
            jnp.asarray(rates),
            jnp.asarray(stokes_table),
            jnp.asarray(swell_table),
        )
        waves, flows = pl.pallas_call(
            lambda *refs: kernel(sections, bands, *refs),
            out_shape=(
                jax.ShapeDtypeStruct((CELLS, SPEC), f32),
                jax.ShapeDtypeStruct((CELLS, 2 * NDEPTH), f32),
            ),
            in_specs=[hbm] * 9,
            out_specs=(vmem, vmem),
            scratch_shapes=[
                pltpu.VMEM((STEPS, CELLS, SPEC), f32),
                pltpu.VMEM((STEPS, CELLS, 128), f32),
                pltpu.VMEM((STEPS, COLS, SPEC), f32),
                pltpu.VMEM((STEPS, COLS, SPEC), f32),
                pltpu.VMEM((STEPS, ROWS, SPEC), f32),
                pltpu.VMEM((STEPS, ROWS, SPEC), f32),
                pltpu.VMEM((STEPS, COLS, 128), f32),
                pltpu.VMEM((STEPS, COLS, 128), f32),
                pltpu.VMEM((STEPS, ROWS, 128), f32),
                pltpu.VMEM((STEPS, ROWS, 128), f32),
                pltpu.VMEM((STEPS, 2, ROWS, SPEC), f32),
                pltpu.VMEM((STEPS, 2, ROWS, 128), f32),
                pltpu.VMEM((2 * STEPS - 1, sections, share, 128), f32),
                pltpu.VMEM((2 * STEPS - 1, sections, share, 128), f32),
                pltpu.VMEM((CELLS, SPEC), f32),
                pltpu.VMEM((STEPS, CELLS, 128), f32),
                pltpu.VMEM((STEPS, CELLS, 128), f32),
                pltpu.VMEM((STEPS, CELLS, 128), f32),
                pltpu.VMEM((ROWS, COLS), f32),
                pltpu.VMEM((ROWS, COLS, 2 * NDEPTH), f32),
                pltpu.VMEM((1, NDEPTH), f32),
                pltpu.VMEM((ROWS, COLS), jnp.int32),
                pltpu.VMEM((ROWS, COLS), jnp.int32),
                pltpu.VMEM((8, SPEC), f32),
                pltpu.VMEM((SPEC, 128), bf16),
                pltpu.VMEM((6 * NDEPTH, SPEC), bf16),
                pltpu.VMEM((4, 8, 128), f32),
                pltpu.VMEM((CELLS, 128), f32),
                pltpu.VMEM((CELLS, 128), f32),
                pltpu.VMEM((CELLS, 128), f32),
                pltpu.SemaphoreType.DMA((9,)),
                pltpu.SemaphoreType.DMA((2 * STEPS, 4)),
                pltpu.SemaphoreType.DMA((2 * STEPS, 4)),
                pltpu.SemaphoreType.DMA((2 * STEPS - 1, sections)),
                pltpu.SemaphoreType.DMA((2 * STEPS - 1, sections)),
            ],
            compiler_params=pltpu.CompilerParams(
                collective_id=0, has_side_effects=True, vmem_limit_bytes=24 << 20
            ),
        )(*[pltpu.with_memory_space_constraint(x, pltpu.HBM) for x in operands])
        waves, flows = pl.pallas_call(
            store,
            out_shape=(
                jax.ShapeDtypeStruct((CELLS, SPEC), f32),
                jax.ShapeDtypeStruct((CELLS, 2 * NDEPTH), f32),
            ),
            in_specs=[vmem, vmem],
            out_specs=(hbm, hbm),
            scratch_shapes=[pltpu.SemaphoreType.DMA((2,))],
        )(*[pltpu.with_memory_space_constraint(x, pltpu.VMEM) for x in (waves, flows)])
        return waves.reshape(ROWS, COLS, SPEC), flows.reshape(ROWS, COLS, 2 * NDEPTH)

    return jax.shard_map(
        per_device,
        mesh=mesh,
        in_specs=(
            P("lat", "sec", None),
            P("lat", "sec"),
            P("lat", "sec", None),
            P(),
            P("lat", "sec"),
            P("lat", "sec"),
        ),
        out_specs=(P("lat", "sec", None), P("lat", "sec", None)),
        check_vma=False,
    )
```

time: 48.2 us -> 39.5 us (0.82)
  the two profiles are of different devices: /device:TPU:64 before, /device:TPU:56 now
where the time goes in v2:
time: 39.5 us; the launch traced here: 39.2 us
  Pallas kernels  38.5 us (97%)
  between operations  0.64 us (2%)
    pallas_call x1, Pallas kernels, per_device(): pl.pallas_call(lambda *refs: kernel(sections, bands, *refs), out_shape=(j...  37.8 us

profile of v2, /device:TPU:56, one launch (start us, length us, event | category | flops | bytes accessed | tf_op | source)
XLA Modules:
  0.0 39.2 jit_solution(12268152846737075674)
XLA Ops:
  0.6 37.8 %shard_map.104 = (f32[96,768]{1,0:T(8,128)S(1)}, f32[96,64]{1,0:T(8,128)S(1)}) custom-call(f32[96,768]{1,0:T(8,128)} %bitcast.4, f32[4,24]{1,0:T(4,128)} %refs_1_.1, f32[4,24,64]{2,1,0:T(8,128)} %refs_2_.1, f32[1,32]{1,0:T(1,128)} %bitcast.5, s32[4,24]{1,0:T(4,128)} %refs_4_.1, s32[4,24]{1,0:T(4,128)} %refs_5_.1, f32[8,768]{1,0:T(8,128)} %constant.6.clone.refs_6_, ...), custom_call_target="tpu_custom_call" | custom-call | tf_op jit(solution)/shard_map/pallas_call | solution.py:486
  38.4 0.7 %shard_map.105 = (f32[96,768]{1,0:T(8,128)}, f32[96,64]{1,0:T(8,128)}) custom-call(f32[96,768]{1,0:T(8,128)S(1)} %get-tuple-element.6.waves_ref, f32[96,64]{1,0:T(8,128)S(1)} %get-tuple-element.7.flows_ref), custom_call_target="tpu_custom_call" | custom-call | tf_op jit(solution)/shard_map/pallas_call | solution.py:535

commit v3 on v2

--- a/solution.py
+++ b/solution.py
@@ -17,7 +17,7 @@
 COLS = 24
 CELLS = ROWS * COLS
 SPEC = NFREQ * NDIR
-WIDE = SPEC + 128
+RING = 3
 
 STOKES_SCALE = 0.1
 OCEAN_DT = 0.3
@@ -101,7 +101,13 @@
     flow_edges,
     outgoing,
     arrived,
+    half_out,
+    half_in,
+    unpacked,
+    edge_lines,
+    band_edges,
     turned,
+    growths,
     spins,
     drifts,
     flow_at_waves,
@@ -130,9 +136,22 @@
     has_west, has_east = sec > 0, sec < sections - 1
     has_south, has_north = lat > 0, lat < bands - 1
 
+    lines = sections // RING
+    line, spot = lax.div(sec, RING), lax.rem(sec, RING)
+    hops = sorted(
+        ((over, along) for over in range(lines) for along in range(RING) if over or along),
+        key=lambda hop: (hop[1] == 0, -min(hop[0], lines - hop[0])),
+    )
+
+    def peer_of(hop):
+        return RING * lax.rem(line + hop[0], lines) + lax.rem(spot + hop[1], RING)
+
+    def source_of(hop):
+        return RING * lax.rem(line + lines - hop[0], lines) + lax.rem(spot + RING - hop[1], RING)
+
     barrier = pltpu.get_barrier_semaphore()
-    for ahead in range(1, sections):
-        peer = lax.rem(sec + ahead, sections)
+    for hop in hops:
+        peer = peer_of(hop)
         pl.semaphore_signal(barrier, inc=1, device_id={"sec": peer}, device_id_type=MESH)
 
     @pl.when(has_south)
@@ -209,9 +228,9 @@
     keep = keep + pltpu.roll(keep, 64, 1)
 
     lane = iota((COLS, 128), 1)
-    line = iota((COLS, 128), 0)
-    first_column = line == 0
-    last_column = line == COLS - 1
+    column = iota((COLS, 128), 0)
+    first_column = column == 0
+    last_column = column == COLS - 1
     direction = lane & (NDIR - 1)
     goes_east = jnp.logical_or(direction < NDIR // 4, direction >= 3 * NDIR // 4)
     goes_north = direction < NDIR // 2
@@ -220,13 +239,18 @@
     full_lane = iota((CELLS, 128), 1)
     low_half = full_lane < 64
     zonal = (full_lane & 63) < 32
+    low_rows = iota((share // 2, 128), 1) < 64
     zonal_row = (lane & 63) < 32
     twist = jnp.where(zonal, OCEAN_DT, -OCEAN_DT)
     global_row = (lat * ROWS).astype(f32)
 
     def halo_copies(step, is_flow):
-        own = (flows if is_flow else waves).at[step]
         edges = (flow_edges if is_flow else wave_edges).at[step]
+        if is_flow:
+            first = flows.at[step, pl.ds(0, COLS)]
+            final = flows.at[step, pl.ds(CELLS - COLS, COLS)]
+        else:
+            first, final = band_edges.at[step, 0], band_edges.at[step, 1]
         south, north, west, east = (
             (flow_south, flow_north, flow_west, flow_east)
             if is_flow
@@ -236,8 +260,8 @@
         plan = (
             (has_west, has_east, edges.at[0], east, {"sec": sec - 1}),
             (has_east, has_west, edges.at[1], west, {"sec": sec + 1}),
-            (has_south, has_north, own.at[pl.ds(0, COLS)], north, {"lat": lat - 1}),
-            (has_north, has_south, own.at[pl.ds(CELLS - COLS, COLS)], south, {"lat": lat + 1}),
+            (has_south, has_north, first, north, {"lat": lat - 1}),
+            (has_north, has_south, final, south, {"lat": lat + 1}),
         )
         for k, (sends, receives, source, halo, device) in enumerate(plan):
             copy = lambda source=source, halo=halo, device=device, k=k: pltpu.make_async_remote_copy(
@@ -250,11 +274,39 @@
             )
             yield sends, receives, copy
 
+    def pack(tiles, needed):
+        return [
+            jnp.where(needed[0 : tiles[0].shape[0]], tiles[2 * c], pltpu.roll(tiles[2 * c + 1], 16, 1))
+            for c in range(SPEC // 256)
+        ]
+
+    def unpack(halo, chunk):
+        return pltpu.roll(halo, 112, 1) if chunk % 2 else halo
+
+    def half_lanes(chunk):
+        return slice(128 * (chunk // 2), 128 * (chunk // 2 + 1))
+
+    def tiles_of(values):
+        return [values[:, 128 * c : 128 * (c + 1)] for c in range(SPEC // 128)]
+
     def send_halos(step, is_flow):
-        own, edges = (flows, flow_edges) if is_flow else (waves, wave_edges)
-        for y in range(ROWS):
-            edges[step, 0, y : y + 1, :] = own[step, COLS * y : COLS * y + 1, :]
-            edges[step, 1, y : y + 1, :] = own[step, COLS * (y + 1) - 1 : COLS * (y + 1), :]
+        if is_flow:
+            for y in range(ROWS):
+                flow_edges[step, 0, y : y + 1, :] = flows[step, COLS * y : COLS * y + 1, :]
+                flow_edges[step, 1, y : y + 1, :] = flows[step, COLS * (y + 1) - 1 : COLS * (y + 1), :]
+        else:
+            for y in range(ROWS):
+                edge_lines[0, y : y + 1, :] = waves[step, COLS * y : COLS * y + 1, :]
+                edge_lines[1, y : y + 1, :] = waves[step, COLS * (y + 1) - 1 : COLS * (y + 1), :]
+            places = (
+                (wave_edges, 0, edge_lines[0], jnp.logical_not(goes_east)),
+                (wave_edges, 1, edge_lines[1], goes_east),
+                (band_edges, 0, waves[step, 0:COLS, :], jnp.logical_not(goes_north)),
+                (band_edges, 1, waves[step, CELLS - COLS : CELLS, :], goes_north),
+            )
+            for edges, side, values, needed in places:
+                for c, tile in enumerate(pack(tiles_of(values), needed)):
+                    edges[step, side, :, 128 * c : 128 * (c + 1)] = tile
         for sends, _, copy in halo_copies(step, is_flow):
 
             @pl.when(sends)
@@ -268,28 +320,61 @@
             def _():
                 copy().wait_recv()
 
-    def pair_copy(index, ahead, source):
-        peer = lax.rem(sec + ahead, sections)
-        slot = lax.rem(sec + sections - ahead, sections) if source else sec
+    def pair_copy(index, k, source):
+        peer = peer_of(hops[k])
+        slot = source_of(hops[k]) if source else sec
         return pltpu.make_async_remote_copy(
-            src_ref=outgoing.at[index, peer],
-            dst_ref=arrived.at[index, slot],
-            send_sem=pair_send.at[index, ahead],
+            src_ref=half_out.at[index - 1, peer] if index else outgoing.at[peer],
+            dst_ref=half_in.at[index - 1, slot] if index else arrived.at[slot],
+            send_sem=pair_send.at[index, k],
             recv_sem=pair_recv.at[index, slot],
             device_id={"sec": peer},
             device_id_type=MESH,
         )
 
+    def start_pairs(index):
+        for k in range(sections - 1):
+            pair_copy(index, k, False).start()
+
+    def send_first(message):
+        outgoing[...] = message.reshape(sections, share, 128)
+        start_pairs(0)
+        arrived[sec] = outgoing[sec]
+
+    def receive(index):
+        for k in range(sections - 1):
+            pair_copy(index, k, True).wait_recv()
+
+    def receive_first():
+        receive(0)
+        return arrived[...].reshape(CELLS, 128)
+
     def send_pairs(index, message):
-        outgoing[index] = message.reshape(sections, share, 128)
-        for ahead in range(1, sections):
-            pair_copy(index, ahead, False).start()
-        arrived[index, sec] = outgoing[index, sec]
+        folded = jnp.where(low_half, message, pltpu.roll(message, CELLS - share // 2, 0))
+        for k in range(sections):
+            half_out[index - 1, k] = folded[share * k : share * k + share // 2, :]
+        start_pairs(index)
+        half_in[index - 1, sec] = half_out[index - 1, sec]
 
     def receive_pairs(index):
-        for ahead in range(1, sections):
-            pair_copy(index, ahead, True).wait_recv()
-        return arrived[index].reshape(CELLS, 128)
+        receive(index)
+        for k in range(sections):
+            rows = half_in[index - 1, k]
+            other = pltpu.roll(rows, 64, 1)
+            unpacked[index - 1, share * k : share * k + share // 2, :] = jnp.where(low_rows, rows, other)
+            unpacked[index - 1, share * k + share // 2 : share * (k + 1), :] = jnp.where(low_rows, other, rows)
+        return unpacked[index - 1]
+
+    def sent_halos(step, is_flow):
+        for sends, _, copy in halo_copies(step, is_flow):
+
+            @pl.when(sends)
+            def _():
+                copy().wait_send()
+
+    def sent_pairs(index):
+        for k in range(sections - 1):
+            pair_copy(index, k, False).wait_send()
 
     def stokes_part(values, chunk):
         high = values.astype(bf16)
@@ -306,16 +391,18 @@
         drift = jnp.dot(place, pieces, preferred_element_type=f32)
         return drift + pltpu.roll(drift, 64, 1)
 
-    def neighbours(own, halos, step, y, lanes):
+    def neighbours(own, halos, step, y, lanes, chunk=None):
         south, north, west, east = halos
         rows = slice(COLS * y, COLS * (y + 1))
         here = own[step, rows, lanes]
+        edge = lanes if chunk is None else half_lanes(chunk)
+        fit = (lambda halo: halo) if chunk is None else (lambda halo: unpack(halo, chunk))
         return (
             here,
-            jnp.where(first_column, west[step, y : y + 1, lanes], pltpu.roll(here, 1, 0)),
-            jnp.where(last_column, east[step, y : y + 1, lanes], pltpu.roll(here, COLS - 1, 0)),
-            own[step, COLS * (y - 1) : COLS * y, lanes] if y else south[step, :, lanes],
-            own[step, COLS * (y + 1) : COLS * (y + 2), lanes] if y < ROWS - 1 else north[step, :, lanes],
+            jnp.where(first_column, fit(west[step, y : y + 1, edge]), pltpu.roll(here, 1, 0)),
+            jnp.where(last_column, fit(east[step, y : y + 1, edge]), pltpu.roll(here, COLS - 1, 0)),
+            own[step, COLS * (y - 1) : COLS * y, lanes] if y else fit(south[step, :, edge]),
+            own[step, COLS * (y + 1) : COLS * (y + 2), lanes] if y < ROWS - 1 else fit(north[step, :, edge]),
         )
 
     def find_spin(step):
@@ -327,7 +414,8 @@
             spin = 0.5 * (sheared + pltpu.roll(sheared, 32, 1))
             spins[step, COLS * y : COLS * (y + 1), :] = spin + (0.2 + 0.6 * (global_row + y) / (ROWS * bands))
 
-    def advect(step):
+    def advect(step, grown=False):
+        drift = None
         for chunk in range(SPEC // 128):
             lanes = slice(128 * chunk, 128 * (chunk + 1))
             stay = rates_ref[0:1, lanes]
@@ -337,7 +425,7 @@
             for y in range(ROWS):
                 rows = slice(COLS * y, COLS * (y + 1))
                 here, west, east, south, north = neighbours(
-                    waves, (wave_south, wave_north, wave_west, wave_east), step, y, lanes
+                    waves, (wave_south, wave_north, wave_west, wave_east), step, y, lanes, chunk
                 )
                 moved = (
                     stay * here
@@ -348,14 +436,27 @@
                 forward = jnp.where(last_direction, pltpu.roll(moved, 31, 1), pltpu.roll(moved, 127, 1))
                 beside = jnp.where(turn_sign[rows, :] > 0.0, behind, forward)
                 rate = turn_size[rows, :] * gain
-                turned[rows, lanes] = (moved + rate * (beside - moved)) * sea[rows, :]
+                moved = (moved + rate * (beside - moved)) * sea[rows, :]
+                if grown:
+                    waves[step + 1, rows, lanes] = moved * growths[rows, lanes]
+                else:
+                    turned[rows, lanes] = moved
+            if grown and chunk % 2:
+                part = stokes_part(waves[step + 1, :, 128 * (chunk - 1) : 128 * (chunk + 1)], chunk // 2)
+                drift = part if drift is None else drift + part
+        return drift
 
     def push(flow, spin, drift, wet):
         return (keep * wet) * (flow + twist * spin * pltpu.roll(flow + drift, 32, 1))
 
+    def find_growth(seen):
+        seen = jnp.concatenate([seen, seen[:, 0:64]], axis=1)
+        for chunk in range(SPEC // 256):
+            lanes = slice(256 * chunk, 256 * (chunk + 1))
+            growths[:, lanes] = 1.0 + jnp.dot(seen, swell_table[:, lanes], preferred_element_type=f32)
+
     def grow(seen, step):
         seen = jnp.concatenate([seen, seen[:, 0:64]], axis=1)
-        drift = None
         for chunk in range(SPEC // 256):
             lanes = slice(256 * chunk, 256 * (chunk + 1))
             growth = jnp.dot(seen, swell_table[:, lanes], preferred_element_type=f32)
@@ -410,7 +511,7 @@
     pl.semaphore_wait(barrier, greeted)
 
     send_halos(0, 1)
-    send_pairs(0, jnp.where(low_half, drift, flows[0]))
+    send_first(jnp.where(low_half, drift, flows[0]))
     send_halos(0, 0)
 
     receive_halos(0, 1)
@@ -418,38 +519,33 @@
     send_pairs(1, spin_message(0))
     receive_halos(0, 0)
     advect(0)
-    message = receive_pairs(0)
+    message = receive_first()
     flows[1] = push(flows[0], spins[0], jnp.where(low_half, message, pltpu.roll(message, 64, 1)), sea[...])
     send_halos(1, 1)
     send_pairs(2, grow(first_seen(message), 1))
 
+    find_growth(next_seen(1, receive_pairs(1)))
     receive_halos(1, 1)
     find_spin(1)
     send_pairs(3, spin_message(1))
     receive_halos(1, 0)
-    advect(1)
-    send_pairs(4, grow(next_seen(1, receive_pairs(1)), 2))
+    drift = advect(1, grown=True)
+    send_halos(2, 0)
+    send_pairs(4, sorted_drift(2, drift))
     flows[2] = push(flows[1], spins[1], receive_pairs(2), sea[...])
     send_halos(2, 1)
 
+    for step in range(STEPS):
+        sent_halos(step, 0)
+        sent_halos(step, 1)
+    for index in range(2 * STEPS - 1):
+        sent_pairs(index)
     receive_halos(2, 0)
     advect(2)
     grow(next_seen(2, receive_pairs(3)), 3)
     receive_halos(2, 1)
     find_spin(2)
     currents_out[...] = push(flows[2], spins[2], receive_pairs(4), sea[...])[:, 0 : 2 * NDEPTH]
-
-    for step in range(STEPS):
-        for is_flow in (0, 1):
-            for sends, _, copy in halo_copies(step, is_flow):
-
-                @pl.when(sends)
-                def _():
-                    copy().wait_send()
-
-    for index in range(2 * STEPS - 1):
-        for ahead in range(1, sections):
-            pair_copy(index, ahead, False).wait_send()
 
 
 def store(waves_ref, flows_ref, waves_out, flows_out, sems):
@@ -494,18 +590,24 @@
             scratch_shapes=[
                 pltpu.VMEM((STEPS, CELLS, SPEC), f32),
                 pltpu.VMEM((STEPS, CELLS, 128), f32),
-                pltpu.VMEM((STEPS, COLS, SPEC), f32),
-                pltpu.VMEM((STEPS, COLS, SPEC), f32),
-                pltpu.VMEM((STEPS, ROWS, SPEC), f32),
-                pltpu.VMEM((STEPS, ROWS, SPEC), f32),
+                pltpu.VMEM((STEPS, COLS, SPEC // 2), f32),
+                pltpu.VMEM((STEPS, COLS, SPEC // 2), f32),
+                pltpu.VMEM((STEPS, ROWS, SPEC // 2), f32),
+                pltpu.VMEM((STEPS, ROWS, SPEC // 2), f32),
                 pltpu.VMEM((STEPS, COLS, 128), f32),
                 pltpu.VMEM((STEPS, COLS, 128), f32),
                 pltpu.VMEM((STEPS, ROWS, 128), f32),
                 pltpu.VMEM((STEPS, ROWS, 128), f32),
-                pltpu.VMEM((STEPS, 2, ROWS, SPEC), f32),
+                pltpu.VMEM((STEPS, 2, ROWS, SPEC // 2), f32),
                 pltpu.VMEM((STEPS, 2, ROWS, 128), f32),
-                pltpu.VMEM((2 * STEPS - 1, sections, share, 128), f32),
-                pltpu.VMEM((2 * STEPS - 1, sections, share, 128), f32),
+                pltpu.VMEM((sections, share, 128), f32),
+                pltpu.VMEM((sections, share, 128), f32),
+                pltpu.VMEM((2 * STEPS - 2, sections, share // 2, 128), f32),
+                pltpu.VMEM((2 * STEPS - 2, sections, share // 2, 128), f32),
+                pltpu.VMEM((2 * STEPS - 2, CELLS, 128), f32),
+                pltpu.VMEM((2, ROWS, SPEC), f32),
+                pltpu.VMEM((STEPS, 2, COLS, SPEC // 2), f32),
+                pltpu.VMEM((CELLS, SPEC), f32),
                 pltpu.VMEM((CELLS, SPEC), f32),
                 pltpu.VMEM((STEPS, CELLS, 128), f32),
                 pltpu.VMEM((STEPS, CELLS, 128), f32),

time: 39.5 us -> 38.1 us (0.965)
  Pallas kernels: 38.5 us -> 36.8 us
    pallas_call x1, Pallas kernels: 37.8 us -> 36.1 us  [per_device(): pl.pallas_call(lambda *refs: kernel(sections, bands, *refs), out_shape=(j...]
where the time goes in v3:
time: 38.1 us; the launch traced here: 37.5 us
  Pallas kernels  36.8 us (97%)
  between operations  0.64 us (2%)
    pallas_call x1, Pallas kernels, per_device(): pl.pallas_call(lambda *refs: kernel(sections, bands, *refs), out_shape=(j...  36.1 us

profile of v3, /device:TPU:56, one launch (start us, length us, event | category | flops | bytes accessed | tf_op | source)
XLA Modules:
  0.0 37.5 jit_solution(525470159204193181)
XLA Ops:
  0.6 36.1 %shard_map.104 = (f32[96,768]{1,0:T(8,128)S(1)}, f32[96,64]{1,0:T(8,128)S(1)}) custom-call(f32[96,768]{1,0:T(8,128)} %bitcast.4, f32[4,24]{1,0:T(4,128)} %refs_1_.1, f32[4,24,64]{2,1,0:T(8,128)} %refs_2_.1, f32[1,32]{1,0:T(1,128)} %bitcast.5, s32[4,24]{1,0:T(4,128)} %refs_4_.1, s32[4,24]{1,0:T(4,128)} %refs_5_.1, f32[8,768]{1,0:T(8,128)} %constant.6.clone.refs_6_, ...), custom_call_target="tpu_custom_call" | custom-call | tf_op jit(solution)/shard_map/pallas_call | solution.py:582
  36.7 0.7 %shard_map.105 = (f32[96,768]{1,0:T(8,128)}, f32[96,64]{1,0:T(8,128)}) custom-call(f32[96,768]{1,0:T(8,128)S(1)} %get-tuple-element.6.waves_ref, f32[96,64]{1,0:T(8,128)S(1)} %get-tuple-element.7.flows_ref), custom_call_target="tpu_custom_call" | custom-call | tf_op jit(solution)/shard_map/pallas_call | solution.py:637

commit v4 on v3

--- a/solution.py
+++ b/solution.py
@@ -146,9 +146,6 @@
     def peer_of(hop):
         return RING * lax.rem(line + hop[0], lines) + lax.rem(spot + hop[1], RING)
 
-    def source_of(hop):
-        return RING * lax.rem(line + lines - hop[0], lines) + lax.rem(spot + RING - hop[1], RING)
-
     barrier = pltpu.get_barrier_semaphore()
     for hop in hops:
         peer = peer_of(hop)
@@ -289,7 +286,7 @@
     def tiles_of(values):
         return [values[:, 128 * c : 128 * (c + 1)] for c in range(SPEC // 128)]
 
-    def send_halos(step, is_flow):
+    def ready_halos(step, is_flow):
         if is_flow:
             for y in range(ROWS):
                 flow_edges[step, 0, y : y + 1, :] = flows[step, COLS * y : COLS * y + 1, :]
@@ -307,6 +304,10 @@
             for edges, side, values, needed in places:
                 for c, tile in enumerate(pack(tiles_of(values), needed)):
                     edges[step, side, :, 128 * c : 128 * (c + 1)] = tile
+
+    def send_halos(step, is_flow, ready=False):
+        if not ready:
+            ready_halos(step, is_flow)
         for sends, _, copy in halo_copies(step, is_flow):
 
             @pl.when(sends)
@@ -320,30 +321,38 @@
             def _():
                 copy().wait_recv()
 
-    def pair_copy(index, k, source):
+    def pair_copy(index, k):
         peer = peer_of(hops[k])
-        slot = source_of(hops[k]) if source else sec
         return pltpu.make_async_remote_copy(
             src_ref=half_out.at[index - 1, peer] if index else outgoing.at[peer],
-            dst_ref=half_in.at[index - 1, slot] if index else arrived.at[slot],
-            send_sem=pair_send.at[index, k],
-            recv_sem=pair_recv.at[index, slot],
+            dst_ref=half_in.at[index - 1, sec] if index else arrived.at[sec],
+            send_sem=pair_send.at[index],
+            recv_sem=pair_recv.at[index],
             device_id={"sec": peer},
             device_id_type=MESH,
         )
 
     def start_pairs(index):
         for k in range(sections - 1):
-            pair_copy(index, k, False).start()
-
-    def send_first(message):
+            pair_copy(index, k).start()
+
+    def ready_first(message):
         outgoing[...] = message.reshape(sections, share, 128)
-        start_pairs(0)
         arrived[sec] = outgoing[sec]
 
+    def all_pairs(index):
+        others = pl.ds(0, sections - 1)
+        return pltpu.make_async_remote_copy(
+            src_ref=half_out.at[index - 1, others] if index else outgoing.at[others],
+            dst_ref=half_in.at[index - 1, others] if index else arrived.at[others],
+            send_sem=pair_send.at[index],
+            recv_sem=pair_recv.at[index],
+            device_id={"sec": peer_of(hops[0])},
+            device_id_type=MESH,
+        )
+
     def receive(index):
-        for k in range(sections - 1):
-            pair_copy(index, k, True).wait_recv()
+        all_pairs(index).wait_recv()
 
     def receive_first():
         receive(0)
@@ -373,8 +382,7 @@
                 copy().wait_send()
 
     def sent_pairs(index):
-        for k in range(sections - 1):
-            pair_copy(index, k, False).wait_send()
+        all_pairs(index).wait_send()
 
     def stokes_part(values, chunk):
         high = values.astype(bf16)
@@ -505,14 +513,16 @@
     flows[0] = jnp.concatenate([start_flow, start_flow], axis=1)
     for load in loads[5:]:
         load.wait()
-    drift = find_drift(0)
+    ready_halos(0, 1)
+    ready_halos(0, 0)
+    ready_first(jnp.where(low_half, find_drift(0), flows[0]))
 
     greeted = sections - 1 + has_south.astype(jnp.int32) + has_north.astype(jnp.int32)
     pl.semaphore_wait(barrier, greeted)
 
-    send_halos(0, 1)
-    send_first(jnp.where(low_half, drift, flows[0]))
-    send_halos(0, 0)
+    start_pairs(0)
+    send_halos(0, 1, ready=True)
+    send_halos(0, 0, ready=True)
 
     receive_halos(0, 1)
     find_spin(0)
@@ -627,8 +637,8 @@
                 pltpu.SemaphoreType.DMA((9,)),
                 pltpu.SemaphoreType.DMA((2 * STEPS, 4)),
                 pltpu.SemaphoreType.DMA((2 * STEPS, 4)),
-                pltpu.SemaphoreType.DMA((2 * STEPS - 1, sections)),
-                pltpu.SemaphoreType.DMA((2 * STEPS - 1, sections)),
+                pltpu.SemaphoreType.DMA((2 * STEPS - 1,)),
+                pltpu.SemaphoreType.DMA((2 * STEPS - 1,)),
             ],
             compiler_params=pltpu.CompilerParams(
                 collective_id=0, has_side_effects=True, vmem_limit_bytes=24 << 20

time: 38.1 us -> 37 us (0.971); the launches traced: 37.5 us -> 36.9 us
  Pallas kernels: 36.8 us -> 36.2 us
    pallas_call x1, Pallas kernels: 36.1 us -> 35.5 us  [per_device(): pl.pallas_call(lambda *refs: kernel(sections, bands, *refs), out_shape=(j...]
where the time goes in v4:
time: 37 us; the launch traced here: 36.9 us
  Pallas kernels  36.2 us (98%)
  between operations  0.64 us (2%)
    pallas_call x1, Pallas kernels, per_device(): pl.pallas_call(lambda *refs: kernel(sections, bands, *refs), out_shape=(j...  35.5 us

profile of v4, /device:TPU:56, one launch (start us, length us, event | category | flops | bytes accessed | tf_op | source)
XLA Modules:
  0.0 36.9 jit_solution(9573937469887497249)
XLA Ops:
  0.6 35.5 %shard_map.104 = (f32[96,768]{1,0:T(8,128)S(1)}, f32[96,64]{1,0:T(8,128)S(1)}) custom-call(f32[96,768]{1,0:T(8,128)} %bitcast.4, f32[4,24]{1,0:T(4,128)} %refs_1_.1, f32[4,24,64]{2,1,0:T(8,128)} %refs_2_.1, f32[1,32]{1,0:T(1,128)} %bitcast.5, s32[4,24]{1,0:T(4,128)} %refs_4_.1, s32[4,24]{1,0:T(4,128)} %refs_5_.1, f32[8,768]{1,0:T(8,128)} %constant.6.clone.refs_6_, ...), custom_call_target="tpu_custom_call" | custom-call | tf_op jit(solution)/shard_map/pallas_call | solution.py:592
  36.2 0.7 %shard_map.105 = (f32[96,768]{1,0:T(8,128)}, f32[96,64]{1,0:T(8,128)}) custom-call(f32[96,768]{1,0:T(8,128)S(1)} %get-tuple-element.6.waves_ref, f32[96,64]{1,0:T(8,128)S(1)} %get-tuple-element.7.flows_ref), custom_call_target="tpu_custom_call" | custom-call | tf_op jit(solution)/shard_map/pallas_call | solution.py:647

commit v5 on v4

--- a/solution.py
+++ b/solution.py
@@ -89,14 +89,10 @@
     currents_out,
     waves,
     flows,
-    wave_south,
-    wave_north,
-    wave_west,
-    wave_east,
-    flow_south,
-    flow_north,
-    flow_west,
-    flow_east,
+    wave_bands,
+    wave_sides,
+    flow_bands,
+    flow_sides,
     wave_edges,
     flow_edges,
     outgoing,
@@ -106,6 +102,8 @@
     unpacked,
     edge_lines,
     band_edges,
+    zeros,
+    no_side,
     turned,
     growths,
     spins,
@@ -144,20 +142,21 @@
     )
 
     def peer_of(hop):
-        return RING * lax.rem(line + hop[0], lines) + lax.rem(spot + hop[1], RING)
+        far, near = line + hop[0], spot + hop[1]
+        far = jnp.where(far >= lines, far - lines, far)
+        return RING * far + jnp.where(near >= RING, near - RING, near)
+
+    peers = [peer_of(hop) for hop in hops]
 
     barrier = pltpu.get_barrier_semaphore()
-    for hop in hops:
-        peer = peer_of(hop)
+    for peer in peers:
         pl.semaphore_signal(barrier, inc=1, device_id={"sec": peer}, device_id_type=MESH)
 
-    @pl.when(has_south)
-    def _():
-        pl.semaphore_signal(barrier, inc=1, device_id={"lat": lat - 1}, device_id_type=MESH)
-
-    @pl.when(has_north)
-    def _():
-        pl.semaphore_signal(barrier, inc=1, device_id={"lat": lat + 1}, device_id_type=MESH)
+    for there, other in ((has_south, lat - 1), (has_north, lat + 1)):
+
+        @pl.when(there)
+        def _():
+            pl.semaphore_signal(barrier, inc=1, device_id={"lat": other}, device_id_type=MESH)
 
     pairs = (
         (turning_hbm, turning_ref),
@@ -174,17 +173,22 @@
     for load in loads:
         load.start()
 
-    for there, halos in (
-        (has_south, (wave_south, flow_south)),
-        (has_north, (wave_north, flow_north)),
-        (has_west, (wave_west, flow_west)),
-        (has_east, (wave_east, flow_east)),
-    ):
-
-        @pl.when(jnp.logical_not(there))
-        def _():
-            for halo in halos:
-                halo[...] = jnp.zeros_like(halo)
+    zeros[...] = jnp.zeros_like(zeros)
+    no_side[...] = jnp.zeros_like(no_side)
+    for step in range(STEPS):
+        for kind, (bands_in, sides_in) in enumerate(((wave_bands, wave_sides), (flow_bands, flow_sides))):
+            width = bands_in.shape[-1]
+            for there, halo, k in (
+                (has_west, sides_in.at[step, 0], 0),
+                (has_east, sides_in.at[step, 1], 0),
+                (has_south, bands_in.at[step, 0], 1),
+                (has_north, bands_in.at[step, 1], 1),
+            ):
+
+                @pl.when(jnp.logical_not(there))
+                def _():
+                    empty = zeros.at[pl.ds(0, COLS), pl.ds(0, width)] if k else no_side.at[:, pl.ds(0, width)]
+                    pltpu.make_async_copy(empty, halo, halo_recv.at[2 * step + kind, k]).start()
 
     tiny[...] = jnp.zeros_like(tiny)
     for load in loads[:4]:
@@ -242,34 +246,29 @@
     global_row = (lat * ROWS).astype(f32)
 
     def halo_copies(step, is_flow):
+        bands_in, sides_in = (flow_bands, flow_sides) if is_flow else (wave_bands, wave_sides)
         edges = (flow_edges if is_flow else wave_edges).at[step]
         if is_flow:
             first = flows.at[step, pl.ds(0, COLS)]
             final = flows.at[step, pl.ds(CELLS - COLS, COLS)]
         else:
             first, final = band_edges.at[step, 0], band_edges.at[step, 1]
-        south, north, west, east = (
-            (flow_south, flow_north, flow_west, flow_east)
-            if is_flow
-            else (wave_south, wave_north, wave_west, wave_east)
-        )
         index = 2 * step + is_flow
         plan = (
-            (has_west, has_east, edges.at[0], east, {"sec": sec - 1}),
-            (has_east, has_west, edges.at[1], west, {"sec": sec + 1}),
-            (has_south, has_north, first, north, {"lat": lat - 1}),
-            (has_north, has_south, final, south, {"lat": lat + 1}),
+            (has_west, edges.at[0], sides_in.at[step, 1], 0, {"sec": sec - 1}),
+            (has_east, edges.at[1], sides_in.at[step, 0], 0, {"sec": sec + 1}),
+            (has_south, first, bands_in.at[step, 1], 1, {"lat": lat - 1}),
+            (has_north, final, bands_in.at[step, 0], 1, {"lat": lat + 1}),
         )
-        for k, (sends, receives, source, halo, device) in enumerate(plan):
-            copy = lambda source=source, halo=halo, device=device, k=k: pltpu.make_async_remote_copy(
+        for number, (there, source, halo, k, device) in enumerate(plan):
+            yield there, lambda: pltpu.make_async_remote_copy(
                 src_ref=source,
-                dst_ref=halo.at[step],
-                send_sem=halo_send.at[index, k],
+                dst_ref=halo,
+                send_sem=halo_send.at[index, number],
                 recv_sem=halo_recv.at[index, k],
                 device_id=device,
                 device_id_type=MESH,
             )
-            yield sends, receives, copy
 
     def pack(tiles, needed):
         return [
@@ -308,21 +307,19 @@
     def send_halos(step, is_flow, ready=False):
         if not ready:
             ready_halos(step, is_flow)
-        for sends, _, copy in halo_copies(step, is_flow):
-
-            @pl.when(sends)
+        for there, copy in halo_copies(step, is_flow):
+
+            @pl.when(there)
             def _():
                 copy().start()
 
     def receive_halos(step, is_flow):
-        for _, receives, copy in halo_copies(step, is_flow):
-
-            @pl.when(receives)
-            def _():
-                copy().wait_recv()
+        for k, halo in enumerate((flow_sides, flow_bands) if is_flow else (wave_sides, wave_bands)):
+            both = halo.at[step]
+            pltpu.make_async_copy(both, both, halo_recv.at[2 * step + is_flow, k]).wait()
 
     def pair_copy(index, k):
-        peer = peer_of(hops[k])
+        peer = peers[k]
         return pltpu.make_async_remote_copy(
             src_ref=half_out.at[index - 1, peer] if index else outgoing.at[peer],
             dst_ref=half_in.at[index - 1, sec] if index else arrived.at[sec],
@@ -347,7 +344,7 @@
             dst_ref=half_in.at[index - 1, others] if index else arrived.at[others],
             send_sem=pair_send.at[index],
             recv_sem=pair_recv.at[index],
-            device_id={"sec": peer_of(hops[0])},
+            device_id={"sec": peers[0]},
             device_id_type=MESH,
         )
 
@@ -375,9 +372,9 @@
         return unpacked[index - 1]
 
     def sent_halos(step, is_flow):
-        for sends, _, copy in halo_copies(step, is_flow):
-
-            @pl.when(sends)
+        for there, copy in halo_copies(step, is_flow):
+
+            @pl.when(there)
             def _():
                 copy().wait_send()
 
@@ -400,24 +397,26 @@
         return drift + pltpu.roll(drift, 64, 1)
 
     def neighbours(own, halos, step, y, lanes, chunk=None):
-        south, north, west, east = halos
+        bands_in, sides_in = halos
         rows = slice(COLS * y, COLS * (y + 1))
         here = own[step, rows, lanes]
         edge = lanes if chunk is None else half_lanes(chunk)
         fit = (lambda halo: halo) if chunk is None else (lambda halo: unpack(halo, chunk))
+        west = fit(sides_in[step, 0, y : y + 1, edge])
+        east = fit(sides_in[step, 1, y : y + 1, edge])
         return (
             here,
-            jnp.where(first_column, fit(west[step, y : y + 1, edge]), pltpu.roll(here, 1, 0)),
-            jnp.where(last_column, fit(east[step, y : y + 1, edge]), pltpu.roll(here, COLS - 1, 0)),
-            own[step, COLS * (y - 1) : COLS * y, lanes] if y else fit(south[step, :, edge]),
-            own[step, COLS * (y + 1) : COLS * (y + 2), lanes] if y < ROWS - 1 else fit(north[step, :, edge]),
+            jnp.where(first_column, west, pltpu.roll(here, 1, 0)),
+            jnp.where(last_column, east, pltpu.roll(here, COLS - 1, 0)),
+            own[step, COLS * (y - 1) : COLS * y, lanes] if y else fit(bands_in[step, 0, :, edge]),
+            own[step, COLS * (y + 1) : COLS * (y + 2), lanes]
+            if y < ROWS - 1
+            else fit(bands_in[step, 1, :, edge]),
         )
 
     def find_spin(step):
         for y in range(ROWS):
-            _, west, east, south, north = neighbours(
-                flows, (flow_south, flow_north, flow_west, flow_east), step, y, slice(0, 128)
-            )
+            _, west, east, south, north = neighbours(flows, (flow_bands, flow_sides), step, y, slice(0, 128))
             sheared = jnp.where(zonal_row, south - north, east - west)
             spin = 0.5 * (sheared + pltpu.roll(sheared, 32, 1))
             spins[step, COLS * y : COLS * (y + 1), :] = spin + (0.2 + 0.6 * (global_row + y) / (ROWS * bands))
@@ -433,7 +432,7 @@
             for y in range(ROWS):
                 rows = slice(COLS * y, COLS * (y + 1))
                 here, west, east, south, north = neighbours(
-                    waves, (wave_south, wave_north, wave_west, wave_east), step, y, lanes, chunk
+                    waves, (wave_bands, wave_sides), step, y, lanes, chunk
                 )
                 moved = (
                     stay * here
@@ -600,14 +599,10 @@
             scratch_shapes=[
                 pltpu.VMEM((STEPS, CELLS, SPEC), f32),
                 pltpu.VMEM((STEPS, CELLS, 128), f32),
-                pltpu.VMEM((STEPS, COLS, SPEC // 2), f32),
-                pltpu.VMEM((STEPS, COLS, SPEC // 2), f32),
-                pltpu.VMEM((STEPS, ROWS, SPEC // 2), f32),
-                pltpu.VMEM((STEPS, ROWS, SPEC // 2), f32),
-                pltpu.VMEM((STEPS, COLS, 128), f32),
-                pltpu.VMEM((STEPS, COLS, 128), f32),
-                pltpu.VMEM((STEPS, ROWS, 128), f32),
-                pltpu.VMEM((STEPS, ROWS, 128), f32),
+                pltpu.VMEM((STEPS, 2, COLS, SPEC // 2), f32),
+                pltpu.VMEM((STEPS, 2, ROWS, SPEC // 2), f32),
+                pltpu.VMEM((STEPS, 2, COLS, 128), f32),
+                pltpu.VMEM((STEPS, 2, ROWS, 128), f32),
                 pltpu.VMEM((STEPS, 2, ROWS, SPEC // 2), f32),
                 pltpu.VMEM((STEPS, 2, ROWS, 128), f32),
                 pltpu.VMEM((sections, share, 128), f32),
@@ -617,6 +612,8 @@
                 pltpu.VMEM((2 * STEPS - 2, CELLS, 128), f32),
                 pltpu.VMEM((2, ROWS, SPEC), f32),
                 pltpu.VMEM((STEPS, 2, COLS, SPEC // 2), f32),
+                pltpu.VMEM((COLS, SPEC // 2), f32),
+                pltpu.VMEM((ROWS, SPEC // 2), f32),
                 pltpu.VMEM((CELLS, SPEC), f32),
                 pltpu.VMEM((CELLS, SPEC), f32),
                 pltpu.VMEM((STEPS, CELLS, 128), f32),
@@ -636,7 +633,7 @@
                 pltpu.VMEM((CELLS, 128), f32),
                 pltpu.SemaphoreType.DMA((9,)),
                 pltpu.SemaphoreType.DMA((2 * STEPS, 4)),
-                pltpu.SemaphoreType.DMA((2 * STEPS, 4)),
+                pltpu.SemaphoreType.DMA((2 * STEPS, 2)),
                 pltpu.SemaphoreType.DMA((2 * STEPS - 1,)),
                 pltpu.SemaphoreType.DMA((2 * STEPS - 1,)),
             ],

time: 37 us -> 37 us (level)
  no operation moved by 1% of the time
where the time goes in v5:
time: 37 us; the launch traced here: 36.9 us
  Pallas kernels  36.2 us (98%)
  between operations  0.64 us (2%)
    pallas_call x1, Pallas kernels, per_device(): pl.pallas_call(lambda *refs: kernel(sections, bands, *refs), out_shape=(j...  35.5 us

profile of v5, /device:TPU:56, one launch (start us, length us, event | category | flops | bytes accessed | tf_op | source)
XLA Modules:
  0.0 36.9 jit_solution(13236049984338571763)
XLA Ops:
  0.6 35.5 %shard_map.104 = (f32[96,768]{1,0:T(8,128)S(1)}, f32[96,64]{1,0:T(8,128)S(1)}) custom-call(f32[96,768]{1,0:T(8,128)} %bitcast.4, f32[4,24]{1,0:T(4,128)} %refs_1_.1, f32[4,24,64]{2,1,0:T(8,128)} %refs_2_.1, f32[1,32]{1,0:T(1,128)} %bitcast.5, s32[4,24]{1,0:T(4,128)} %refs_4_.1, s32[4,24]{1,0:T(4,128)} %refs_5_.1, f32[8,768]{1,0:T(8,128)} %constant.6.clone.refs_6_, ...), custom_call_target="tpu_custom_call" | custom-call | tf_op jit(solution)/shard_map/pallas_call | solution.py:591
  36.1 0.7 %shard_map.105 = (f32[96,768]{1,0:T(8,128)}, f32[96,64]{1,0:T(8,128)}) custom-call(f32[96,768]{1,0:T(8,128)S(1)} %get-tuple-element.6.waves_ref, f32[96,64]{1,0:T(8,128)S(1)} %get-tuple-element.7.flows_ref), custom_call_target="tpu_custom_call" | custom-call | tf_op jit(solution)/shard_map/pallas_call | solution.py:644

commit v6 on v5

--- a/solution.py
+++ b/solution.py
@@ -18,6 +18,7 @@
 CELLS = ROWS * COLS
 SPEC = NFREQ * NDIR
 RING = 3
+SIDES, BANDS = slice(0, 2), slice(2, 4)
 
 STOKES_SCALE = 0.1
 OCEAN_DT = 0.3
@@ -261,7 +262,7 @@
             (has_north, final, bands_in.at[step, 0], 1, {"lat": lat + 1}),
         )
         for number, (there, source, halo, k, device) in enumerate(plan):
-            yield there, lambda: pltpu.make_async_remote_copy(
+            yield there, lambda source=source, halo=halo, device=device, k=k, number=number: pltpu.make_async_remote_copy(
                 src_ref=source,
                 dst_ref=halo,
                 send_sem=halo_send.at[index, number],
@@ -285,7 +286,7 @@
     def tiles_of(values):
         return [values[:, 128 * c : 128 * (c + 1)] for c in range(SPEC // 128)]
 
-    def ready_halos(step, is_flow):
+    def ready_sides(step, is_flow):
         if is_flow:
             for y in range(ROWS):
                 flow_edges[step, 0, y : y + 1, :] = flows[step, COLS * y : COLS * y + 1, :]
@@ -294,24 +295,35 @@
             for y in range(ROWS):
                 edge_lines[0, y : y + 1, :] = waves[step, COLS * y : COLS * y + 1, :]
                 edge_lines[1, y : y + 1, :] = waves[step, COLS * (y + 1) - 1 : COLS * (y + 1), :]
-            places = (
-                (wave_edges, 0, edge_lines[0], jnp.logical_not(goes_east)),
-                (wave_edges, 1, edge_lines[1], goes_east),
-                (band_edges, 0, waves[step, 0:COLS, :], jnp.logical_not(goes_north)),
-                (band_edges, 1, waves[step, CELLS - COLS : CELLS, :], goes_north),
-            )
-            for edges, side, values, needed in places:
-                for c, tile in enumerate(pack(tiles_of(values), needed)):
-                    edges[step, side, :, 128 * c : 128 * (c + 1)] = tile
+            for side, needed in ((0, jnp.logical_not(goes_east)), (1, goes_east)):
+                for c, tile in enumerate(pack(tiles_of(edge_lines[side]), needed)):
+                    wave_edges[step, side, :, 128 * c : 128 * (c + 1)] = tile
+
+    def ready_bands(step, is_flow):
+        if not is_flow:
+            for side, needed in ((0, jnp.logical_not(goes_north)), (1, goes_north)):
+                rows = slice(side * (CELLS - COLS), side * (CELLS - COLS) + COLS)
+                for c, tile in enumerate(pack(tiles_of(waves[step, rows, :]), needed)):
+                    band_edges[step, side, :, 128 * c : 128 * (c + 1)] = tile
+
+    def ready_halos(step, is_flow):
+        ready_sides(step, is_flow)
+        ready_bands(step, is_flow)
+
+    def start_halos(step, is_flow, part):
+        for sends, copy in list(halo_copies(step, is_flow))[part]:
+
+            @pl.when(sends)
+            def _():
+                copy().start()
 
     def send_halos(step, is_flow, ready=False):
         if not ready:
-            ready_halos(step, is_flow)
-        for there, copy in halo_copies(step, is_flow):
-
-            @pl.when(there)
-            def _():
-                copy().start()
+            ready_sides(step, is_flow)
+        start_halos(step, is_flow, SIDES)
+        if not ready:
+            ready_bands(step, is_flow)
+        start_halos(step, is_flow, BANDS)
 
     def receive_halos(step, is_flow):
         for k, halo in enumerate((flow_sides, flow_bands) if is_flow else (wave_sides, wave_bands)):
@@ -329,8 +341,10 @@
             device_id_type=MESH,
         )
 
-    def start_pairs(index):
-        for k in range(sections - 1):
+    far, near = range(sections - lines), range(sections - lines, sections - 1)
+
+    def start_pairs(index, which=None):
+        for k in range(sections - 1) if which is None else which:
             pair_copy(index, k).start()
 
     def ready_first(message):
@@ -355,11 +369,11 @@
         receive(0)
         return arrived[...].reshape(CELLS, 128)
 
-    def send_pairs(index, message):
+    def send_pairs(index, message, which=None):
         folded = jnp.where(low_half, message, pltpu.roll(message, CELLS - share // 2, 0))
         for k in range(sections):
             half_out[index - 1, k] = folded[share * k : share * k + share // 2, :]
-        start_pairs(index)
+        start_pairs(index, which)
         half_in[index - 1, sec] = half_out[index - 1, sec]
 
     def receive_pairs(index):
@@ -519,9 +533,12 @@
     greeted = sections - 1 + has_south.astype(jnp.int32) + has_north.astype(jnp.int32)
     pl.semaphore_wait(barrier, greeted)
 
-    start_pairs(0)
-    send_halos(0, 1, ready=True)
-    send_halos(0, 0, ready=True)
+    start_pairs(0, far)
+    start_halos(0, 1, SIDES)
+    start_halos(0, 0, SIDES)
+    start_pairs(0, near)
+    start_halos(0, 1, BANDS)
+    start_halos(0, 0, BANDS)
 
     receive_halos(0, 1)
     find_spin(0)
@@ -536,10 +553,11 @@
     find_growth(next_seen(1, receive_pairs(1)))
     receive_halos(1, 1)
     find_spin(1)
-    send_pairs(3, spin_message(1))
+    send_pairs(3, spin_message(1), far)
     receive_halos(1, 0)
     drift = advect(1, grown=True)
     send_halos(2, 0)
+    start_pairs(3, near)
     send_pairs(4, sorted_drift(2, drift))
     flows[2] = push(flows[1], spins[1], receive_pairs(2), sea[...])
     send_halos(2, 1)

time: 37 us -> 37 us (level)
  no operation moved by 1% of the time
where the time goes in v6:
time: 37 us; the launch traced here: 36.7 us
  Pallas kernels  36.1 us (98%)
  between operations  0.64 us (2%)
    pallas_call x1, Pallas kernels, per_device(): pl.pallas_call(lambda *refs: kernel(sections, bands, *refs), out_shape=(j...  35.4 us

profile of v6, /device:TPU:56, one launch (start us, length us, event | category | flops | bytes accessed | tf_op | source)
XLA Modules:
  0.0 36.7 jit_solution(13757233248184220715)
XLA Ops:
  0.6 35.4 %shard_map.104 = (f32[96,768]{1,0:T(8,128)S(1)}, f32[96,64]{1,0:T(8,128)S(1)}) custom-call(f32[96,768]{1,0:T(8,128)} %bitcast.4, f32[4,24]{1,0:T(4,128)} %refs_1_.1, f32[4,24,64]{2,1,0:T(8,128)} %refs_2_.1, f32[1,32]{1,0:T(1,128)} %bitcast.5, s32[4,24]{1,0:T(4,128)} %refs_4_.1, s32[4,24]{1,0:T(4,128)} %refs_5_.1, f32[8,768]{1,0:T(8,128)} %constant.6.clone.refs_6_, ...), custom_call_target="tpu_custom_call" | custom-call | tf_op jit(solution)/shard_map/pallas_call | solution.py:609
  36.0 0.7 %shard_map.105 = (f32[96,768]{1,0:T(8,128)}, f32[96,64]{1,0:T(8,128)}) custom-call(f32[96,768]{1,0:T(8,128)S(1)} %get-tuple-element.6.waves_ref, f32[96,64]{1,0:T(8,128)S(1)} %get-tuple-element.7.flows_ref), custom_call_target="tpu_custom_call" | custom-call | tf_op jit(solution)/shard_map/pallas_call | solution.py:662

commit v7 on v5

--- a/solution.py
+++ b/solution.py
@@ -444,11 +444,13 @@
                 beside = jnp.where(turn_sign[rows, :] > 0.0, behind, forward)
                 rate = turn_size[rows, :] * gain
                 moved = (moved + rate * (beside - moved)) * sea[rows, :]
-                if grown:
+                if grown and step == STEPS - 1:
+                    spectra_out[rows, lanes] = moved * growths[rows, lanes]
+                elif grown:
                     waves[step + 1, rows, lanes] = moved * growths[rows, lanes]
                 else:
                     turned[rows, lanes] = moved
-            if grown and chunk % 2:
+            if grown and chunk % 2 and step < STEPS - 1:
                 part = stokes_part(waves[step + 1, :, 128 * (chunk - 1) : 128 * (chunk + 1)], chunk // 2)
                 drift = part if drift is None else drift + part
         return drift
@@ -549,9 +551,9 @@
         sent_halos(step, 1)
     for index in range(2 * STEPS - 1):
         sent_pairs(index)
+    find_growth(next_seen(2, receive_pairs(3)))
     receive_halos(2, 0)
-    advect(2)
-    grow(next_seen(2, receive_pairs(3)), 3)
+    advect(2, grown=True)
     receive_halos(2, 1)
     find_spin(2)
     currents_out[...] = push(flows[2], spins[2], receive_pairs(4), sea[...])[:, 0 : 2 * NDEPTH]

time: 37 us -> 37.7 us (1.019)
  Pallas kernels: 36.2 us -> 36.9 us
    pallas_call x1, Pallas kernels: 35.5 us -> 36.1 us  [per_device(): pl.pallas_call(lambda *refs: kernel(sections, bands, *refs), out_shape=(j...]
where the time goes in v7:
time: 37.7 us; the launch traced here: 37.5 us
  Pallas kernels  36.9 us (98%)
  between operations  0.64 us (2%)
    pallas_call x1, Pallas kernels, per_device(): pl.pallas_call(lambda *refs: kernel(sections, bands, *refs), out_shape=(j...  36.1 us

profile of v7, /device:TPU:56, one launch (start us, length us, event | category | flops | bytes accessed | tf_op | source)
XLA Modules:
  0.0 37.5 jit_solution(1678931573018586115)
XLA Ops:
  0.6 36.1 %shard_map.104 = (f32[96,768]{1,0:T(8,128)S(1)}, f32[96,64]{1,0:T(8,128)S(1)}) custom-call(f32[96,768]{1,0:T(8,128)} %bitcast.4, f32[4,24]{1,0:T(4,128)} %refs_1_.1, f32[4,24,64]{2,1,0:T(8,128)} %refs_2_.1, f32[1,32]{1,0:T(1,128)} %bitcast.5, s32[4,24]{1,0:T(4,128)} %refs_4_.1, s32[4,24]{1,0:T(4,128)} %refs_5_.1, f32[8,768]{1,0:T(8,128)} %constant.6.clone.refs_6_, ...), custom_call_target="tpu_custom_call" | custom-call | tf_op jit(solution)/shard_map/pallas_call | solution.py:593
  36.8 0.7 %shard_map.105 = (f32[96,768]{1,0:T(8,128)}, f32[96,64]{1,0:T(8,128)}) custom-call(f32[96,768]{1,0:T(8,128)S(1)} %get-tuple-element.6.waves_ref, f32[96,64]{1,0:T(8,128)S(1)} %get-tuple-element.7.flows_ref), custom_call_target="tpu_custom_call" | custom-call | tf_op jit(solution)/shard_map/pallas_call | solution.py:646
